TPU v7x, 32 devices: a whole 2x2x4 slice. The times are simulated.
32 devices in a mesh: rows: 8 (over y, x, core), cols: 4 (over z).
Axes of the slice: x: 2, y: 2, z: 4, core: 2. Of those that a mesh axis runs over, the one named last changes fastest.
Arguments:
- matrix: float32 [4096, 4096], P('rows', 'cols'), may hold values from -24 to 24
- gap_table: float32 [2, 2048, 256], P(None, 'rows'), may hold values from 8 to 32
- orders: int32 [2, 8, 2], replicated, may hold values from 0 to 1, each once within a row
Outputs:
- result: float32 [4096, 4096], P('rows', 'cols')
Inputs may be any that keep to these rules, and one draw needn't show every extreme that they name: `orders`: each pair's two entries are 0 and 1 in some order.
All inputs are finite; a program needn't handle non-finite values.
Results may differ from a plain program's by a relative error of at most 0.00029.
Values sent between devices are 32-bit elements; how exact they have to be, the bound alone decides.
No kernel may reach another device: no remote copies, remote signals or barrier semaphores. Data moves between devices by JAX's collectives and lax.ppermute only.
A program may use at most 64 MiB of HBM per device.

v0:
```python
import functools
import jax
import jax.numpy as jnp
from jax import lax
from jax.experimental import pallas as pl
from jax.experimental.pallas import tpu as pltpu
from jax.sharding import PartitionSpec as P


F32 = jnp.float32
BF16 = jnp.bfloat16
HIGHEST = lax.Precision.HIGHEST
EASY_NORM = 8.0
KERNEL_BYTES = 20 << 20

ANY = pl.BlockSpec(memory_space=pl.ANY)
VMEM = pl.BlockSpec(memory_space=pltpu.VMEM)
SMEM = pl.BlockSpec(memory_space=pltpu.SMEM)
HBM = pl.BlockSpec(memory_space=pltpu.HBM)


def split(value):
    high = value.astype(BF16)
    low = (value - high.astype(F32)).astype(BF16)
    return high, low


def coarse_dot(left, right):
    return jnp.dot(left.astype(BF16), right.astype(BF16), preferred_element_type=F32)


def fine_dot(left, right):
    (left_high, left_low), (right_high, right_low) = left, right
    wide = jnp.concatenate([left_high, left_high, left_low], axis=1)
    tall = jnp.concatenate([right_high, right_low, right_high], axis=0)
    return jnp.dot(wide, tall, preferred_element_type=F32)


def full_dot(left, right):
    return jnp.dot(left, right, precision=HIGHEST, preferred_element_type=F32)


def factors(ref, index):
    return tuple((ref[index, 2 * part], ref[index, 2 * part + 1]) for part in range(3))


def turn_rows(first, second, parts):
    plain, flipped, weight = parts
    mixed = fine_dot(flipped, split(first)) + second
    image = 2.0 * fine_dot(weight, split(mixed))
    return first - fine_dot(plain, split(image)), image - second


def turn_columns(first, second, parts):
    plain, flipped, weight = parts
    mixed = fine_dot(split(first), plain) + second
    image = 2.0 * fine_dot(split(mixed), weight)
    return first - fine_dot(split(image), flipped), image - second


def eye(width):
    shape = (width, width)
    return (lax.broadcasted_iota(jnp.int32, shape, 0) == lax.broadcasted_iota(jnp.int32, shape, 1)).astype(F32)


def row_sums(value):
    return jnp.max(jnp.sum(jnp.abs(value), axis=0, keepdims=True), axis=1, keepdims=True)


def invert(generators, weights):
    count, width = generators.shape[0], generators.shape[1]
    identity = eye(width)
    every = range(count)
    shifted = [identity + fine_dot(split(generators[q].T), split(generators[q])) for q in every]
    square = [coarse_dot(m, m) for m in shifted]
    bounds = [jnp.sqrt(row_sums(square[q]) + 0.01 * row_sums(shifted[q]) ** 2) for q in every]
    worst = bounds[0]
    for bound in bounds[1:]:
        worst = jnp.maximum(worst, bound)
    norm = jnp.max(worst)

    @pl.when(norm <= EASY_NORM)
    def _():
        guess, rest, grow = [], [], []
        for q in every:
            bound = jnp.maximum(bounds[q], 1.25)
            ratio = (bound + 1.0) / (bound - 1.0)
            two = 2.0 * ratio * ratio - 1.0
            four = 2.0 * two * two - 1.0
            eight = 2.0 * four * four - 1.0
            scale = 8.0 / (two * (bound - 1.0) * (bound - 1.0))
            guess.append((scale * (bound + 1.0)) * identity - scale * shifted[q])
            rest.append(identity - (scale * (bound + 1.0)) * shifted[q] + scale * square[q])
            grow.append((2.0 * two * two / four, 1.0 / four, 2.0 * four * four / eight))
        both = [coarse_dot(jnp.concatenate([guess[q], rest[q]], axis=0), rest[q]) for q in every]
        guess = [grow[q][0] * (guess[q] + both[q][:width]) for q in every]
        rest = [grow[q][0] * both[q][width:] - grow[q][1] * identity for q in every]
        step = [coarse_dot(guess[q], rest[q]) for q in every]
        guess = [grow[q][2] * (guess[q] + step[q]) for q in every]
        rest = [identity - fine_dot(split(shifted[q]), split(guess[q])) for q in every]
        for q in every:
            weights[q] = guess[q] + coarse_dot(guess[q], rest[q])

    @pl.when(norm > EASY_NORM)
    def _():
        rounds = jnp.int32(10)
        for power in range(30):
            rounds += (norm > EASY_NORM * 2.0**power).astype(jnp.int32)

        def solve(q, carry):
            plain = generators[q]
            system = identity + full_dot(plain.T, plain)
            weights[q] = (2.0 / (1.0 + jnp.max(row_sums(system)))) * identity

            def improve(_, carry):
                guess = weights[q]
                weights[q] = guess + full_dot(guess, identity - full_dot(system, guess))
                return carry

            return lax.fori_loop(0, rounds, improve, carry)

        lax.fori_loop(0, count, solve, 0)


def places(shape):
    rows, cols = shape
    band_pairs = rows // cols
    row, col = lax.axis_index("rows"), lax.axis_index("cols")
    return row, col, lax.div(row, band_pairs), lax.rem(row, band_pairs)


def copies_of(pairs, sems):
    copies = [pltpu.make_async_copy(source, target, sems.at[index]) for index, (source, target) in enumerate(pairs)]
    for copy in copies:
        copy.start()
    return copies


def wait_all(copies):
    for copy in copies:
        copy.wait()


def first_generators_kernel(shape, matrix, gap_table, out, coupling, gap, sems):
    width = out.shape[0]
    _, col, group, lane = places(shape)
    anchor = pl.multiple_of(lane * (2 * width) + width, width)
    wait_all(copies_of([(matrix.at[pl.ds(0, width), pl.ds(anchor, width)], coupling), (gap_table.at[0], gap)], sems))
    out[...] = jnp.where(group == col, coupling[...] / (2.0 * gap[...]), 0.0)


def find_factors(shape, carried, parts, factor_out, generators, weights):
    band_pairs = shape[0] // shape[1]
    lane = places(shape)[3]
    generators[0] = parts[0][...] + parts[1][...]
    for shift, part in enumerate(parts[2:]):
        generators[1 + lax.rem(lane + carried - shift + band_pairs, band_pairs)] = part[...]
    invert(generators, weights)
    for index in range(1 + band_pairs):
        plain = generators[index]
        for part, value in enumerate((plain, plain.T, weights[index])):
            factor_out[index, 2 * part], factor_out[index, 2 * part + 1] = split(value)


def weights_kernel(shape, carried, *refs):
    find_factors(shape, carried, refs[:-3], *refs[-3:])


def weights_and_next_kernel(shape, step, carried, *refs):
    rows, cols = shape
    band_pairs = rows // cols
    orders, matrix, own_gap, next_gap = refs[:4]
    factor_out, row_out, band_out, generators, weights = refs[6 + band_pairs :]
    width = row_out.shape[0]
    row, col, _, _ = places(shape)
    before, after = lax.rem(row - 1 + rows, rows), lax.rem(row + 1, rows)
    find_factors(shape, carried, refs[4 : 6 + band_pairs], factor_out, generators, weights)

    def coupling(pair, row_flag, col_flag):
        cols = pl.ds(pl.multiple_of(pair * (2 * width), 2 * width), 2 * width)
        top, bottom = turn_rows(matrix[:width, cols], matrix[width:, cols], factors(factor_out, 0))
        picked = jnp.where(row_flag == 0, top, bottom)
        left, right = turn_columns(picked[:, :width], picked[:, width:], factors(factor_out, 1 + pair))
        return jnp.where(col_flag == 0, left, right)

    row_here, band_here = lax.div(before, band_pairs) == col, lax.div(after, band_pairs) == col

    @pl.when(row_here)
    def _():
        found = coupling(lax.rem(before, band_pairs), orders[step, row, 0], orders[step, before, 1])
        row_out[...] = found / (2.0 * own_gap[step + 1])

    @pl.when(jnp.logical_not(row_here))
    def _():
        row_out[...] = jnp.zeros_like(row_out)

    @pl.when(band_here)
    def _():
        found = coupling(lax.rem(after, band_pairs), orders[step, row, 1], orders[step, after, 0])
        band_out[...] = found.T / (2.0 * next_gap[...])

    @pl.when(jnp.logical_not(band_here))
    def _():
        band_out[...] = jnp.zeros_like(band_out)


def rotate_kernel(shape, step, pairs, quarters, *refs):
    count = 1 + max(quarter[0] for corners in quarters for quarter in corners)
    orders, factor_in, outputs = refs[0], refs[1 + count], refs[2 + count :]
    band_pairs = shape[0] // shape[1]
    width = factor_in.shape[2]
    row, col, _, _ = places(shape)
    own = factors(factor_in, 0)
    keep_rows = orders[step, row, 0] == 0
    for index, (pair, corners) in enumerate(zip(pairs, quarters)):
        tiles = [refs[1 + which][pl.ds(at_row, width), pl.ds(at_col, width)] for which, at_row, at_col in corners]
        first, second = jnp.concatenate(tiles[:2], axis=1), jnp.concatenate(tiles[2:], axis=1)
        top, bottom = turn_rows(first, second, own)
        parts = factors(factor_in, 1 + pair)
        keep_cols = orders[step, col * band_pairs + pair, 0] == 0
        for leaves in (0, 1):
            picked = jnp.where(keep_rows, bottom, top) if leaves else jnp.where(keep_rows, top, bottom)
            left, right = turn_columns(picked[:, :width], picked[:, width:], parts)
            stay, away = jnp.where(keep_cols, left, right), jnp.where(keep_cols, right, left)
            if pair == band_pairs - 1:
                outputs[leaves][...], outputs[2 + leaves][...] = stay, away
            else:
                outputs[leaves][:, pl.ds(2 * index * width, width)] = stay
                outputs[leaves][:, pl.ds((2 * index + 1) * width, width)] = away


def local_fill_kernel(width, last_stay, others, out, sems):
    band = others.shape[1] // (2 * width)
    moves = [(last_stay, 2 * band)]
    for pair in range(band):
        moves.append((others.at[:, pl.ds(2 * pair * width, width)], 2 * pair))
        moves.append((others.at[:, pl.ds((2 * pair + 1) * width, width)], 2 * pair + 3))
    wait_all(copies_of([(source, out.at[pl.ds(0, width), pl.ds(slot * width, width)]) for source, slot in moves], sems))


def fill_kernel(width, partial, last_in, others_in, col_in, corner_in, out, sems):
    del partial
    band = others_in.shape[1] // (2 * width)
    moves = [(col_in, 0, 1), (corner_in, width, 1), (last_in, width, 2 * band)]
    for pair in range(band):
        moves.append((others_in.at[:, pl.ds(2 * pair * width, width)], width, 2 * pair))
        moves.append((others_in.at[:, pl.ds((2 * pair + 1) * width, width)], width, 2 * pair + 3))
    wait_all(
        copies_of(
            [(source, out.at[pl.ds(at_row, width), pl.ds(slot * width, width)]) for source, at_row, slot in moves], sems
        )
    )


def send(value, pairs):
    return lax.ppermute(value, ("rows", "cols"), pairs)


def bits_below(count):
    return [1 << bit for bit in range((count - 1).bit_length())]


def row_rounds(shape, carried):
    rows, cols = shape
    band_pairs = rows // cols
    held, rounds = [0], []

    def device(row, moved):
        return row * cols + ((row - carried) % rows // band_pairs ^ moved)

    for bit in reversed(bits_below(cols)):
        rounds.append([(device(row, d), device(row, d ^ bit)) for row in range(rows) for d in held])
        held = held + [d ^ bit for d in held]
    return rounds


def band_rounds(shape, carried):
    rows, cols = shape
    band_pairs = rows // cols
    held, rounds = [0], []

    def device(col, lane, moved):
        start = (col - (carried and lane == band_pairs - 1)) % cols
        return ((start ^ moved) * band_pairs + lane) * cols + col

    for bit in bits_below(cols) if carried else reversed(bits_below(cols)):
        rounds.append(
            [
                (device(col, lane, d), device(col, lane, d ^ bit))
                for col in range(cols)
                for d in held
                for lane in range(band_pairs)
            ]
        )
        held = held + [d ^ bit for d in held]
    return rounds


def within_group(value, shape, shift):
    rows, cols = shape
    band_pairs = rows // cols
    return lax.ppermute(
        value,
        "rows",
        [(row, row // band_pairs * band_pairs + (row + shift) % band_pairs) for row in range(rows)],
    )


def to_next_rows(value, shape):
    return lax.ppermute(value, "rows", [(r, (r + 1) % shape[0]) for r in range(shape[0])])


def to_next_cols(value, shape):
    return lax.ppermute(value, "cols", [(c, (c + 1) % shape[1]) for c in range(shape[1])])


def to_next_corner(value, shape):
    rows, cols = shape
    return send(
        value, [(r * cols + c, (r + 1) % rows * cols + (c + 1) % cols) for r in range(rows) for c in range(cols)]
    )


def placed(value, space):
    return value if space is None else pltpu.with_memory_space_constraint(value, space)


def call(kernel, outputs, operands, scratch=(), specs=None, **settings):
    specs = specs or {}
    spaces = {id(SMEM): None, id(ANY): None, id(HBM): pltpu.HBM}
    operands = [placed(value, spaces[id(specs[index])] if index in specs else pltpu.VMEM) for index, value in enumerate(operands)]
    return pl.pallas_call(
        kernel,
        out_shape=outputs,
        in_specs=[specs.get(index, VMEM) for index in range(len(operands))],
        out_specs=settings.pop("out_specs", jax.tree.map(lambda _: VMEM, outputs)),
        scratch_shapes=list(scratch),
        compiler_params=pltpu.CompilerParams(vmem_limit_bytes=KERNEL_BYTES),
        **settings,
    )(*operands)


def spread(row_value, band_value, shape, carried):
    row_held, band_held, row_late, band_late = row_value, band_value, None, None
    for row_pairs, band_pairs in zip(row_rounds(shape, carried), band_rounds(shape, carried)):
        if row_late is not None:
            row_held, band_held = row_held + row_late, band_held + band_late
        band_late = send(band_held, band_pairs)
        row_late = send(row_held, row_pairs)
    band_held = band_held + band_late
    lanes = shape[0] // shape[1]
    return [row_held, row_late, band_held] + [within_group(band_held, shape, shift) for shift in range(1, lanes)]


def finish(pieces, width, tall, wide):
    last_stay, others, last_in, others_in, col_in, corner_in = pieces
    result = jax.ShapeDtypeStruct((tall, wide), F32)
    count = wide // width
    partial = call(
        functools.partial(local_fill_kernel, width),
        result,
        (last_stay, others),
        [pltpu.SemaphoreType.DMA((count,))],
        out_specs=ANY,
    )
    return call(
        functools.partial(fill_kernel, width),
        result,
        (partial, last_in, others_in, col_in, corner_in),
        [pltpu.SemaphoreType.DMA((count + 2,))],
        specs={0: ANY},
        out_specs=ANY,
        input_output_aliases={0: 0},
    )


def shards(shape, matrix, gap_table, orders):
    rows, cols = shape
    band_pairs = rows // cols
    width = gap_table.shape[2]
    steps = orders.shape[0]
    tall, wide = matrix.shape
    square = pltpu.VMEM((width, width), F32)
    many = pltpu.VMEM((width, wide - 2 * width), F32)
    stack = pltpu.VMEM((1 + band_pairs, width, width), F32)
    split_stack = pltpu.VMEM((1 + band_pairs, 6, width, width), BF16)
    dma = pltpu.SemaphoreType.DMA

    row_value = call(
        functools.partial(first_generators_kernel, shape),
        square,
        (matrix, gap_table),
        [square, square, dma((2,))],
        specs={0: HBM, 1: HBM},
    )
    band_value = row_value

    last_pair = band_pairs - 1
    for step in range(steps):
        carried = int(step > 0)
        parts = spread(row_value, band_value, shape, carried)
        if step == steps - 1:
            split_factors = call(functools.partial(weights_kernel, shape, carried), split_stack, parts, [stack, stack])
        else:
            if step > 0:
                matrix = finish(pieces, width, tall, wide)
            wanted = [
                ((row + 1) % rows * cols + (row + 1) % rows // band_pairs, row * cols + (row + 1) % rows // band_pairs)
                for row in range(rows)
            ]
            next_gap = send(gap_table[step + 1], wanted)
            split_factors, row_value, band_value = call(
                functools.partial(weights_and_next_kernel, shape, step, carried),
                (split_stack, square, square),
                (orders, matrix, gap_table, next_gap, *parts),
                [stack, stack],
                specs={0: SMEM},
            )
        if step < steps - 1 or steps == 1:
            tiles = lambda pair: tuple((0, i * width, (2 * pair + j) * width) for i in (0, 1) for j in (0, 1))
            last_inputs, last_tiles = (matrix,), (tiles(last_pair),)
            other_inputs, other_tiles = (matrix,), tuple(tiles(pair) for pair in range(last_pair))
        else:
            last_stay, others, last_in, others_in, col_in, corner_in = pieces
            last_inputs = (last_stay, others, last_in, others_in)
            edge = (2 * last_pair - 1) * width
            last_tiles = (((0, 0, 0), (1, 0, edge), (2, 0, 0), (3, 0, edge)),)
            other_inputs = (others, others_in, col_in, corner_in)
            other_tiles = tuple(
                tuple(
                    (side, 0, 2 * pair * width) if slot == 0 else (side, 0, (2 * pair - 1) * width) if pair else (2 + side, 0, 0)
                    for side in (0, 1)
                    for slot in (0, 1)
                )
                for pair in range(last_pair)
            )
        last_stay, last_leave, col_piece, corner_piece = call(
            functools.partial(rotate_kernel, shape, step, (last_pair,), last_tiles),
            (square,) * 4,
            (orders, *last_inputs, split_factors),
            specs={0: SMEM},
        )
        others, others_leave = call(
            functools.partial(rotate_kernel, shape, step, tuple(range(last_pair)), other_tiles),
            (many, many),
            (orders, *other_inputs, split_factors),
            specs={0: SMEM},
        )
        col_in = to_next_cols(col_piece, shape)
        corner_in = to_next_corner(corner_piece, shape)
        last_in = to_next_rows(last_leave, shape)
        others_in = to_next_rows(others_leave, shape)
        pieces = (last_stay, others, last_in, others_in, col_in, corner_in)
    return finish(pieces, width, tall, wide)


def solution(mesh):
    shape = (mesh.shape["rows"], mesh.shape["cols"])
    in_specs = (P("rows", "cols"), P(None, "rows", None), P())
    out_specs = P("rows", "cols")

    def body(matrix, gap_table, orders):
        return shards(shape, matrix, gap_table, orders)

    return jax.shard_map(body, mesh=mesh, in_specs=in_specs, out_specs=out_specs, check_vma=False)
```

profile of v0, /device:TPU:0, one launch (start us, length us, event | category | flops | bytes accessed | tf_op | source)
XLA Modules:
  0.0 171.1 jit_solution(2331404762236928302)
XLA Ops:
  0.0 0.0 copy-start
  0.0 0.0 copy-start.1
  0.0 0.0 copy-start.2
  0.0 1.2 shard_map.37
  1.3 4.9 %collective-permute-start.3 = (f32[256,256]{1,0:T(8,128)S(1)}, f32[256,256]{1,0:T(8,128)S(1)}, u32[]{:S(2)}, u32[]{:S(2)}) collective-permute-start(f32[256,256]{1,0:T(8,128)S(1)} %shard_map.37), channel_id=1, source_target_pairs={{0,16},{4,20},{9,25},{13,29},{18,2},{22,6},{27,11},{31,15}} | collective-permute-start | bytes 786440 | tf_op jit(solution)/shard_map/ppermute | solution.py:256
  6.2 2.4 %collective-permute-start.1 = (f32[256,256]{1,0:T(8,128)S(1)}, f32[256,256]{1,0:T(8,128)S(1)}, u32[]{:S(2)}, u32[]{:S(2)}) collective-permute-start(f32[256,256]{1,0:T(8,128)S(1)} %shard_map.37), channel_id=1, source_target_pairs={{0,2},{4,6},{9,11},{13,15},{18,16},{22,20},{27,25},{31,29}} | collective-permute-start | bytes 786440 | tf_op jit(solution)/shard_map/ppermute | solution.py:256
  8.6 3.2 %collective-permute-done.3 = f32[256,256]{1,0:T(8,128)S(1)} collective-permute-done((f32[256,256]{1,0:T(8,128)S(1)}, f32[256,256]{1,0:T(8,128)S(1)}, u32[]{:S(2)}, u32[]{:S(2)}) %collective-permute-start.3) | collective-permute-done | bytes 262176 | tf_op jit(solution)/shard_map/ppermute | solution.py:256
  11.7 2.4 %collective-permute-done.1 = f32[256,256]{1,0:T(8,128)S(1)} collective-permute-done((f32[256,256]{1,0:T(8,128)S(1)}, f32[256,256]{1,0:T(8,128)S(1)}, u32[]{:S(2)}, u32[]{:S(2)}) %collective-permute-start.1) | collective-permute-done | bytes 262176 | tf_op jit(solution)/shard_map/ppermute | solution.py:256
  14.1 0.1 fusion
  14.2 1.3 collective-permute-start.4
  15.5 0.0 copy-done.1
  15.5 0.7 slice_bitcast_fusion
  16.2 1.9 %collective-permute-start = (f32[256,256]{1,0:T(8,128)}, f32[256,256]{1,0:T(8,128)S(1)}, u32[]{:S(2)}, u32[]{:S(2)}) collective-permute-start(f32[256,256]{1,0:T(8,128)} %slice_bitcast_fusion), channel_id=1, source_target_pairs={{4,0},{9,5},{13,9},{18,14},{22,18},{27,23},{31,27},{0,28}} | collective-permute-start | bytes 786440 | tf_op jit(solution)/shard_map/ppermute | solution.py:256
  18.1 2.0 %collective-permute-start.2 = (f32[256,256]{1,0:T(8,128)S(1)}, f32[256,256]{1,0:T(8,128)}, u32[]{:S(2)}, u32[]{:S(2)}) collective-permute-start(f32[256,256]{1,0:T(8,128)S(1)} %get-tuple-element.36.refs_4_), channel_id=1, source_target_pairs={{0,1},{2,3},{4,5},{6,7},{9,8},{11,10},{13,12},{15,14},{18,19},{16,... | collective-permute-start | bytes 786440 | tf_op jit(solution)/shard_map/ppermute | solution.py:256
  20.1 0.3 collective-permute-done.4
  20.5 0.3 collective-permute-start.5
  20.7 0.0 copy-done.2
  20.7 0.1 copy.8.refs_0_
  20.8 2.5 %collective-permute-done.refs_3_ = f32[256,256]{1,0:T(8,128)S(1)} collective-permute-done((f32[256,256]{1,0:T(8,128)}, f32[256,256]{1,0:T(8,128)S(1)}, u32[]{:S(2)}, u32[]{:S(2)}) %collective-permute-start) | collective-permute-done | bytes 262176 | tf_op jit(solution)/shard_map/ppermute | solution.py:256
  23.3 2.6 %collective-permute-done.2.refs_5_ = f32[256,256]{1,0:T(8,128)} collective-permute-done((f32[256,256]{1,0:T(8,128)S(1)}, f32[256,256]{1,0:T(8,128)}, u32[]{:S(2)}, u32[]{:S(2)}) %collective-permute-start.2) | collective-permute-done | bytes 262176 | tf_op jit(solution)/shard_map/ppermute | solution.py:256
  25.9 0.0 collective-permute-done.5.refs_7_
  25.9 0.0 copy-done
  25.9 45.5 %shard_map.38 = (bf16[3,6,256,256]{3,2,1,0:T(8,128)(2,1)S(1)}, f32[256,256]{1,0:T(8,128)S(1)}, f32[256,256]{1,0:T(8,128)S(1)}) custom-call(s32[2,8,2]{2,1,0:T(8,128)S(1)} %copy.8.refs_0_, f32[512,1024]{1,0:T(8,128)S(1)} %copy-done, f32[2,256,256]{2,1,0:T(8,128)S(1)} %copy-done.1, f32[256,256]{1,0:T(8,128)S(1)} %collective-permute-done.refs_3_, ...), custom_call_target="tpu_custom_call" | custom-call | tf_op jit(solution)/shard_map/pallas_call | solution.py:332
  71.5 5.5 %collective-permute-start.10 = (f32[256,256]{1,0:T(8,128)S(1)}, f32[256,256]{1,0:T(8,128)S(1)}, u32[]{:S(2)}, u32[]{:S(2)}) collective-permute-start(f32[256,256]{1,0:T(8,128)S(1)} %get-tuple-element.26), channel_id=1, source_target_pairs={{0,8},{28,20},{9,1},{5,13},{18,26},{14,6},{27,19},{23,31}} | collective-permute-start | bytes 786440 | tf_op jit(solution)/shard_map/ppermute | solution.py:256
  76.9 0.7 collective-permute-start.8
  77.6 3.2 %collective-permute-done.10 = f32[256,256]{1,0:T(8,128)S(1)} collective-permute-done((f32[256,256]{1,0:T(8,128)S(1)}, f32[256,256]{1,0:T(8,128)S(1)}, u32[]{:S(2)}, u32[]{:S(2)}) %collective-permute-start.10) | collective-permute-done | bytes 262176 | tf_op jit(solution)/shard_map/ppermute | solution.py:256
  80.8 1.3 collective-permute-start.11
  82.2 3.1 %shard_map.40 = (f32[256,512]{1,0:T(8,128)S(1)}, f32[256,512]{1,0:T(8,128)S(1)}) custom-call(s32[2,8,2]{2,1,0:T(8,128)S(1)} %copy.8.refs_0_, f32[512,1024]{1,0:T(8,128)S(1)} %copy-done, bf16[3,6,256,256]{3,2,1,0:T(8,128)(2,1)S(1)} %get-tuple-element.20.refs_2_), custom_call_target="tpu_custom_call" | custom-call | tf_op jit(solution)/shard_map/pallas_call | solution.py:332
  85.3 0.1 collective-permute-start.7
  85.3 3.1 %shard_map.39 = (f32[256,256]{1,0:T(8,128)S(1)}, f32[256,256]{1,0:T(8,128)S(1)}, f32[256,256]{1,0:T(8,128)S(1)}, f32[256,256]{1,0:T(8,128)S(1)}) custom-call(s32[2,8,2]{2,1,0:T(8,128)S(1)} %copy.8.refs_0_, f32[512,1024]{1,0:T(8,128)S(1)} %copy-done, bf16[3,6,256,256]{3,2,1,0:T(8,128)(2,1)S(1)} %get-tuple-element.20.refs_2_), custom_call_target="tpu_custom_call" | custom-call | tf_op jit(solution)/shard_map/pallas_call | solution.py:332
  88.4 0.0 collective-permute-done.8
  88.5 1.3 collective-permute-start.9
  89.8 0.0 collective-permute-done.11
  89.8 2.7 %collective-permute-start.12 = (f32[256,256]{1,0:T(8,128)S(1)}, f32[256,256]{1,0:T(8,128)S(1)}, u32[]{:S(2)}, u32[]{:S(2)}) collective-permute-start(f32[256,256]{1,0:T(8,128)S(1)} %add.23.refs_2_), channel_id=1, source_target_pairs={{0,4},{4,0},{8,12},{12,8},{16,20},{20,16},{24,28},{28,24},{1,5},{5... | collective-permute-start | bytes 786440 | tf_op jit(solution)/shard_map/ppermute | solution.py:302
  92.5 0.1 collective-permute-start.13
  92.6 0.1 collective-permute-start.14
  92.7 4.1 %collective-permute-done.9.refs_1_ = f32[256,256]{1,0:T(8,128)S(1)} collective-permute-done((f32[256,256]{1,0:T(8,128)S(1)}, f32[256,256]{1,0:T(8,128)S(1)}, u32[]{:S(2)}, u32[]{:S(2)}) %collective-permute-start.9) | collective-permute-done | bytes 262176 | tf_op jit(solution)/shard_map/ppermute | solution.py:256
  96.7 0.7 collective-permute-start.6
  97.5 0.0 collective-permute-done.12.refs_3_
  97.5 39.4 %shard_map.41.refs_5_ = bf16[3,6,256,256]{3,2,1,0:T(8,128)(2,1)S(1)} custom-call(f32[256,256]{1,0:T(8,128)S(1)} %add.21.refs_0_, f32[256,256]{1,0:T(8,128)S(1)} %collective-permute-done.9.refs_1_, f32[256,256]{1,0:T(8,128)S(1)} %add.23.refs_2_, f32[256,256]{1,0:T(8,128)S(1)} %collective-permute-done.12.refs_3_), custom_call_target="tpu_custom_call" | custom-call | tf_op jit(solution)/shard_map/pallas_call | solution.py:332
  136.9 0.0 collective-permute-done.13.refs_3_
  136.9 0.0 collective-permute-done.14.refs_4_
  136.9 0.0 collective-permute-done.7.refs_4_.refs_2_
  136.9 3.1 %shard_map.43 = (f32[256,512]{1,0:T(8,128)S(1)}, f32[256,512]{1,0:T(8,128)S(1)}) custom-call(s32[2,8,2]{2,1,0:T(8,128)S(1)} %copy.8.refs_0_, f32[256,512]{1,0:T(8,128)S(1)} %get-tuple-element.22.refs_2_.refs_1_, f32[256,512]{1,0:T(8,128)S(1)} %collective-permute-done.7.refs_4_.refs_2_, f32[256,256]{1,0:T(8,128)S(1)} %collective-permute-done.13.refs_3_, ...), custom_call_target="tpu_custom_call" | custom-call | tf_op jit(solution)/shard_map/pallas_call | solution.py:332
  140.0 1.6 collective-permute-start.16
  141.6 0.0 collective-permute-done.6.refs_3_
  141.6 3.1 %shard_map.42 = (f32[256,256]{1,0:T(8,128)S(1)}, f32[256,256]{1,0:T(8,128)S(1)}, f32[256,256]{1,0:T(8,128)S(1)}, f32[256,256]{1,0:T(8,128)S(1)}) custom-call(s32[2,8,2]{2,1,0:T(8,128)S(1)} %copy.8.refs_0_, f32[256,256]{1,0:T(8,128)S(1)} %get-tuple-element.21.refs_1_, f32[256,512]{1,0:T(8,128)S(1)} %get-tuple-element.22.refs_2_.refs_1_, ...), custom_call_target="tpu_custom_call" | custom-call | tf_op jit(solution)/shard_map/pallas_call | solution.py:332
  144.8 0.1 collective-permute-start.15
  144.8 2.5 %collective-permute-start.17 = (f32[256,256]{1,0:T(8,128)S(1)}, f32[256,256]{1,0:T(8,128)S(1)}, u32[]{:S(2)}, u32[]{:S(2)}) collective-permute-start(f32[256,256]{1,0:T(8,128)S(1)} %get-tuple-element.33), channel_id=1, source_target_pairs={{0,1},{1,2},{2,3},{3,0},{4,5},{5,6},{6,7},{7,4},{8,9},{9,10},{10,1... | collective-permute-start | bytes 786440 | tf_op jit(solution)/shard_map/ppermute | solution.py:314
  147.3 0.0 collective-permute-start.18
  147.4 0.9 shard_map.44.partial
  148.3 13.5 %collective-permute-done.15.last_in = f32[256,256]{1,0:T(8,128)S(1)} collective-permute-done((f32[256,256]{1,0:T(8,128)S(1)}, f32[256,256]{1,0:T(8,128)S(1)}, u32[]{:S(2)}, u32[]{:S(2)}) %collective-permute-start.15) | collective-permute-done | bytes 262176 | tf_op jit(solution)/shard_map/ppermute | solution.py:310
  161.7 0.0 collective-permute-done.17.col_in
  161.7 8.1 %collective-permute-done.18.corner_in = f32[256,256]{1,0:T(8,128)S(1)} collective-permute-done((f32[256,256]{1,0:T(8,128)S(1)}, f32[256,256]{1,0:T(8,128)S(1)}, u32[]{:S(2)}, u32[]{:S(2)}) %collective-permute-start.18) | collective-permute-done | bytes 262176 | tf_op jit(solution)/shard_map/ppermute | solution.py:256
  169.8 0.0 collective-permute-done.16.others_in
  169.8 1.1 shard_map.45
  (4 shorter events, 0.1 us)
Async XLA Ops:
  0.0 25.9 %copy-start = (f32[512,1024]{1,0:T(8,128)S(1)}, f32[512,1024]{1,0:T(8,128)}, u32[]{:S(2)}) copy-start(f32[512,1024]{1,0:T(8,128)} %refs_1_.5) | copy-start | bytes 6291460
  0.0 15.5 %copy-start.1 = (f32[2,256,256]{2,1,0:T(8,128)S(1)}, f32[2,256,256]{2,1,0:T(8,128)}, u32[]{:S(2)}) copy-start(f32[2,256,256]{2,1,0:T(8,128)} %refs_2_.1) | copy-start | bytes 1572868
  0.0 20.7 %copy-start.2 = (s32[2,8,2]{1,2,0:T(2,128)S(1)}, s32[2,8,2]{1,2,0:T(2,128)}, u32[]{:S(2)}) copy-start(s32[2,8,2]{1,2,0:T(2,128)} %param.5) | copy-start | bytes 388
  1.3 10.5 %collective-permute-start.3 = (f32[256,256]{1,0:T(8,128)S(1)}, f32[256,256]{1,0:T(8,128)S(1)}, u32[]{:S(2)}, u32[]{:S(2)}) collective-permute-start(f32[256,256]{1,0:T(8,128)S(1)} %shard_map.37), channel_id=1, source_target_pairs={{0,16},{4,20},{9,25},{13,29},{18,2},{22,6},{27,11},{31,15}} | collective-permute-start | bytes 786440 | tf_op jit(solution)/shard_map/ppermute | solution.py:256
  6.2 7.9 %collective-permute-start.1 = (f32[256,256]{1,0:T(8,128)S(1)}, f32[256,256]{1,0:T(8,128)S(1)}, u32[]{:S(2)}, u32[]{:S(2)}) collective-permute-start(f32[256,256]{1,0:T(8,128)S(1)} %shard_map.37), channel_id=1, source_target_pairs={{0,2},{4,6},{9,11},{13,15},{18,16},{22,20},{27,25},{31,29}} | collective-permute-start | bytes 786440 | tf_op jit(solution)/shard_map/ppermute | solution.py:256
  14.2 6.3 %collective-permute-start.4 = (f32[256,256]{1,0:T(8,128)S(1)}, f32[256,256]{1,0:T(8,128)S(1)}, u32[]{:S(2)}, u32[]{:S(2)}) collective-permute-start(f32[256,256]{1,0:T(8,128)S(1)} %get-tuple-element.35), channel_id=1, source_target_pairs={{0,8},{4,12},{16,24},{20,28},{9,1},{13,5},{25,17},{29,21},{18,26},... | collective-permute-start | bytes 786440 | tf_op jit(solution)/shard_map/ppermute | solution.py:256
  16.2 7.1 %collective-permute-start = (f32[256,256]{1,0:T(8,128)}, f32[256,256]{1,0:T(8,128)S(1)}, u32[]{:S(2)}, u32[]{:S(2)}) collective-permute-start(f32[256,256]{1,0:T(8,128)} %slice_bitcast_fusion), channel_id=1, source_target_pairs={{4,0},{9,5},{13,9},{18,14},{22,18},{27,23},{31,27},{0,28}} | collective-permute-start | bytes 786440 | tf_op jit(solution)/shard_map/ppermute | solution.py:256
  18.1 7.8 %collective-permute-start.2 = (f32[256,256]{1,0:T(8,128)S(1)}, f32[256,256]{1,0:T(8,128)}, u32[]{:S(2)}, u32[]{:S(2)}) collective-permute-start(f32[256,256]{1,0:T(8,128)S(1)} %get-tuple-element.36.refs_4_), channel_id=1, source_target_pairs={{0,1},{2,3},{4,5},{6,7},{9,8},{11,10},{13,12},{15,14},{18,19},{16,... | collective-permute-start | bytes 786440 | tf_op jit(solution)/shard_map/ppermute | solution.py:256
  20.5 5.5 %collective-permute-start.5 = (f32[256,256]{1,0:T(8,128)S(1)}, f32[256,256]{1,0:T(8,128)}, u32[]{:S(2)}, u32[]{:S(2)}) collective-permute-start(f32[256,256]{1,0:T(8,128)S(1)} %add.20.refs_6_), channel_id=1, source_target_pairs={{0,4},{4,0},{8,12},{12,8},{16,20},{20,16},{24,28},{28,24},{1,5},{5... | collective-permute-start | bytes 786440 | tf_op jit(solution)/shard_map/ppermute | solution.py:302
  71.5 9.3 %collective-permute-start.10 = (f32[256,256]{1,0:T(8,128)S(1)}, f32[256,256]{1,0:T(8,128)S(1)}, u32[]{:S(2)}, u32[]{:S(2)}) collective-permute-start(f32[256,256]{1,0:T(8,128)S(1)} %get-tuple-element.26), channel_id=1, source_target_pairs={{0,8},{28,20},{9,1},{5,13},{18,26},{14,6},{27,19},{23,31}} | collective-permute-start | bytes 786440 | tf_op jit(solution)/shard_map/ppermute | solution.py:256
  76.9 11.5 %collective-permute-start.8 = (f32[256,256]{1,0:T(8,128)S(1)}, f32[256,256]{1,0:T(8,128)S(1)}, u32[]{:S(2)}, u32[]{:S(2)}) collective-permute-start(f32[256,256]{1,0:T(8,128)S(1)} %get-tuple-element.25), channel_id=1, source_target_pairs={{3,1},{4,6},{8,10},{13,15},{17,19},{22,20},{26,24},{31,29}} | collective-permute-start | bytes 786440 | tf_op jit(solution)/shard_map/ppermute | solution.py:256
  80.8 8.9 %collective-permute-start.11 = (f32[256,256]{1,0:T(8,128)S(1)}, f32[256,256]{1,0:T(8,128)S(1)}, u32[]{:S(2)}, u32[]{:S(2)}) collective-permute-start(f32[256,256]{1,0:T(8,128)S(1)} %add.22), channel_id=1, source_target_pairs={{0,16},{28,12},{8,24},{20,4},{9,25},{5,21},{1,17},{13,29},{18,2},{... | collective-permute-start | bytes 786440 | tf_op jit(solution)/shard_map/ppermute | solution.py:256
  85.3 51.7 %collective-permute-start.7 = (f32[256,512]{1,0:T(8,128)S(1)}, f32[256,512]{1,0:T(8,128)S(1)}, u32[]{:S(2)}, u32[]{:S(2)}) collective-permute-start(f32[256,512]{1,0:T(8,128)S(1)} %get-tuple-element.24), channel_id=1, source_target_pairs={{0,4},{4,8},{8,12},{12,16},{16,20},{20,24},{24,28},{28,0},{1,5},{5... | collective-permute-start | bytes 1572872 | tf_op jit(solution)/shard_map/ppermute | solution.py:310
  88.5 8.3 %collective-permute-start.9 = (f32[256,256]{1,0:T(8,128)S(1)}, f32[256,256]{1,0:T(8,128)S(1)}, u32[]{:S(2)}, u32[]{:S(2)}) collective-permute-start(f32[256,256]{1,0:T(8,128)S(1)} %add.21.refs_0_), channel_id=1, source_target_pairs={{3,2},{1,0},{4,5},{6,7},{8,9},{10,11},{13,12},{15,14},{17,16},{19,... | collective-permute-start | bytes 786440 | tf_op jit(solution)/shard_map/ppermute | solution.py:256
  89.8 7.7 %collective-permute-start.12 = (f32[256,256]{1,0:T(8,128)S(1)}, f32[256,256]{1,0:T(8,128)S(1)}, u32[]{:S(2)}, u32[]{:S(2)}) collective-permute-start(f32[256,256]{1,0:T(8,128)S(1)} %add.23.refs_2_), channel_id=1, source_target_pairs={{0,4},{4,0},{8,12},{12,8},{16,20},{20,16},{24,28},{28,24},{1,5},{5... | collective-permute-start | bytes 786440 | tf_op jit(solution)/shard_map/ppermute | solution.py:302
  92.5 44.4 %collective-permute-start.13 = (f32[256,256]{1,0:T(8,128)S(1)}, f32[256,256]{1,0:T(8,128)S(1)}, u32[]{:S(2)}, u32[]{:S(2)}) collective-permute-start(f32[256,256]{1,0:T(8,128)S(1)} %get-tuple-element.28), channel_id=1, source_target_pairs={{0,1},{1,2},{2,3},{3,0},{4,5},{5,6},{6,7},{7,4},{8,9},{9,10},{10,1... | collective-permute-start | bytes 786440 | tf_op jit(solution)/shard_map/ppermute | solution.py:314
  92.6 44.3 %collective-permute-start.14 = (f32[256,256]{1,0:T(8,128)S(1)}, f32[256,256]{1,0:T(8,128)S(1)}, u32[]{:S(2)}, u32[]{:S(2)}) collective-permute-start(f32[256,256]{1,0:T(8,128)S(1)} %get-tuple-element.29), channel_id=1, source_target_pairs={{0,5},{1,6},{2,7},{3,4},{4,9},{5,10},{6,11},{7,8},{8,13},{9,14},{1... | collective-permute-start | bytes 786440 | tf_op jit(solution)/shard_map/ppermute | solution.py:256
  96.7 44.9 %collective-permute-start.6 = (f32[256,256]{1,0:T(8,128)S(1)}, f32[256,256]{1,0:T(8,128)S(1)}, u32[]{:S(2)}, u32[]{:S(2)}) collective-permute-start(f32[256,256]{1,0:T(8,128)S(1)} %get-tuple-element.23), channel_id=1, source_target_pairs={{0,4},{4,8},{8,12},{12,16},{16,20},{20,24},{24,28},{28,0},{1,5},{5... | collective-permute-start | bytes 786440 | tf_op jit(solution)/shard_map/ppermute | solution.py:310
  140.0 29.8 %collective-permute-start.16 = (f32[256,512]{1,0:T(8,128)S(1)}, f32[256,512]{1,0:T(8,128)S(1)}, u32[]{:S(2)}, u32[]{:S(2)}) collective-permute-start(f32[256,512]{1,0:T(8,128)S(1)} %get-tuple-element.32), channel_id=1, source_target_pairs={{0,4},{4,8},{8,12},{12,16},{16,20},{20,24},{24,28},{28,0},{1,5},{5... | collective-permute-start | bytes 1572872 | tf_op jit(solution)/shard_map/ppermute | solution.py:310
  144.8 17.0 %collective-permute-start.15 = (f32[256,256]{1,0:T(8,128)S(1)}, f32[256,256]{1,0:T(8,128)S(1)}, u32[]{:S(2)}, u32[]{:S(2)}) collective-permute-start(f32[256,256]{1,0:T(8,128)S(1)} %get-tuple-element.31), channel_id=1, source_target_pairs={{0,4},{4,8},{8,12},{12,16},{16,20},{20,24},{24,28},{28,0},{1,5},{5... | collective-permute-start | bytes 786440 | tf_op jit(solution)/shard_map/ppermute | solution.py:310
  144.8 16.9 %collective-permute-start.17 = (f32[256,256]{1,0:T(8,128)S(1)}, f32[256,256]{1,0:T(8,128)S(1)}, u32[]{:S(2)}, u32[]{:S(2)}) collective-permute-start(f32[256,256]{1,0:T(8,128)S(1)} %get-tuple-element.33), channel_id=1, source_target_pairs={{0,1},{1,2},{2,3},{3,0},{4,5},{5,6},{6,7},{7,4},{8,9},{9,10},{10,1... | collective-permute-start | bytes 786440 | tf_op jit(solution)/shard_map/ppermute | solution.py:314
  147.3 22.4 %collective-permute-start.18 = (f32[256,256]{1,0:T(8,128)S(1)}, f32[256,256]{1,0:T(8,128)S(1)}, u32[]{:S(2)}, u32[]{:S(2)}) collective-permute-start(f32[256,256]{1,0:T(8,128)S(1)} %get-tuple-element.34), channel_id=1, source_target_pairs={{0,5},{1,6},{2,7},{3,4},{4,9},{5,10},{6,11},{7,8},{8,13},{9,14},{1... | collective-permute-start | bytes 786440 | tf_op jit(solution)/shard_map/ppermute | solution.py:256
where the time goes:
time: 171 us
  Pallas kernels  101 us (59%)
  waiting for transfers between devices  39.7 us (23%)
  starting transfers between devices  29.4 us (17%)
    pallas_call x9, Pallas kernels, call(): pl.pallas_call(kernel, out_shape=outputs, in_specs=[specs.get(index, VMEM...  101 us
    ppermute x11, waiting for transfers between devices, send(): return lax.ppermute(value, ('rows', 'cols'), pairs)  26.3 us
    ppermute x11, starting transfers between devices, send(): return lax.ppermute(value, ('rows', 'cols'), pairs)  21.3 us
    ppermute x4, waiting for transfers between devices, to_next_rows(): lax.ppermute(value, 'rows', [(r, (r + 1) % shape[0]) for r in range(shape...  13.5 us
  transfers between devices with their start and end apart: 19, of which 9 were waited for; matrix products, arithmetic and copies ran while one was open for 1% of the time, Pallas kernels for 31%

commit v1 on v0

--- a/solution.py
+++ b/solution.py
@@ -218,15 +218,19 @@
         top, bottom = turn_rows(first, second, own)
         parts = factors(factor_in, 1 + pair)
         keep_cols = orders[step, col * band_pairs + pair, 0] == 0
+        first = jnp.concatenate([top[:, :width], bottom[:, :width]], axis=0)
+        second = jnp.concatenate([top[:, width:], bottom[:, width:]], axis=0)
+        left, right = turn_columns(first, second, parts)
+        stay, away = jnp.where(keep_cols, left, right), jnp.where(keep_cols, right, left)
         for leaves in (0, 1):
-            picked = jnp.where(keep_rows, bottom, top) if leaves else jnp.where(keep_rows, top, bottom)
-            left, right = turn_columns(picked[:, :width], picked[:, width:], parts)
-            stay, away = jnp.where(keep_cols, left, right), jnp.where(keep_cols, right, left)
+            keep = jnp.logical_not(keep_rows) if leaves else keep_rows
+            stay_rows = jnp.where(keep, stay[:width], stay[width:])
+            away_rows = jnp.where(keep, away[:width], away[width:])
             if pair == band_pairs - 1:
-                outputs[leaves][...], outputs[2 + leaves][...] = stay, away
+                outputs[leaves][...], outputs[2 + leaves][...] = stay_rows, away_rows
             else:
-                outputs[leaves][:, pl.ds(2 * index * width, width)] = stay
-                outputs[leaves][:, pl.ds((2 * index + 1) * width, width)] = away
+                outputs[leaves][:, pl.ds(2 * index * width, width)] = stay_rows
+                outputs[leaves][:, pl.ds((2 * index + 1) * width, width)] = away_rows
 
 
 def local_fill_kernel(width, last_stay, others, out, sems):
@@ -277,22 +281,16 @@
 def band_rounds(shape, carried):
     rows, cols = shape
     band_pairs = rows // cols
-    held, rounds = [0], []
-
-    def device(col, lane, moved):
-        start = (col - (carried and lane == band_pairs - 1)) % cols
-        return ((start ^ moved) * band_pairs + lane) * cols + col
-
-    for bit in bits_below(cols) if carried else reversed(bits_below(cols)):
-        rounds.append(
-            [
-                (device(col, lane, d), device(col, lane, d ^ bit))
-                for col in range(cols)
-                for d in held
-                for lane in range(band_pairs)
-            ]
-        )
-        held = held + [d ^ bit for d in held]
+    bits = bits_below(cols)
+    rounds = [[] for _ in bits]
+    for lane in range(band_pairs):
+        order = bits[lane % len(bits) :] + bits[: lane % len(bits)]
+        for col in range(cols):
+            start = (col - (carried and lane == band_pairs - 1)) % cols
+            held = [start]
+            for pairs, bit in zip(rounds, order):
+                pairs.extend(((g * band_pairs + lane) * cols + col, ((g ^ bit) * band_pairs + lane) * cols + col) for g in held)
+                held = held + [g ^ bit for g in held]
     return rounds
 
 
@@ -393,7 +391,7 @@
         [square, square, dma((2,))],
         specs={0: HBM, 1: HBM},
     )
-    band_value = row_value
+    band_value = lax.optimization_barrier(row_value)
 
     last_pair = band_pairs - 1
     for step in range(steps):

time: 171 us -> 166 us (0.971)
  waiting for transfers between devices: 39.7 us -> 36.1 us
    ppermute x11, waiting for transfers between devices: 26.3 us -> 22 us  [send(): return lax.ppermute(value, ('rows', 'cols'), pairs)]
    ppermute x2, starting transfers between devices: 2.92 us -> 0.3 us  [within_group(): lax.ppermute(value, 'rows', [(row, row // band_pairs * band_pairs + (row...]
    ppermute x11, starting transfers between devices: 21.3 us -> 23.1 us  [send(): return lax.ppermute(value, ('rows', 'cols'), pairs)]
  transfers between devices with their start and end apart: 19 -> 19, of which waited for: 9 -> 8; matrix products, arithmetic and copies ran while one was open for 1% -> 1% of each run, Pallas kernels for 31% -> 31%
where the time goes in v1:
time: 166 us; the launch traced here: 165 us
  Pallas kernels  99.3 us (60%)
  waiting for transfers between devices  36.1 us (22%)
  starting transfers between devices  28.5 us (17%)
    pallas_call x9, Pallas kernels, call(): pl.pallas_call(kernel, out_shape=outputs, in_specs=[specs.get(index, VMEM...  99.3 us
    ppermute x11, starting transfers between devices, send(): return lax.ppermute(value, ('rows', 'cols'), pairs)  23.1 us
    ppermute x11, waiting for transfers between devices, send(): return lax.ppermute(value, ('rows', 'cols'), pairs)  22 us
    ppermute x4, waiting for transfers between devices, to_next_rows(): lax.ppermute(value, 'rows', [(r, (r + 1) % shape[0]) for r in range(shape...  14.1 us
  transfers between devices with their start and end apart: 19, of which 8 were waited for; matrix products, arithmetic and copies ran while one was open for 1% of the time, Pallas kernels for 31%

profile of v1, /device:TPU:0, one launch (start us, length us, event | category | flops | bytes accessed | tf_op | source)
XLA Modules:
  0.0 165.3 jit_solution(12601018759728860723)
XLA Ops:
  0.0 0.0 copy-start.1
  0.0 1.1 shard_map.37
  1.2 0.0 copy-start.2
  1.2 0.0 copy-start
  1.2 5.0 %collective-permute-start.3 = (f32[256,256]{1,0:T(8,128)S(1)}, f32[256,256]{1,0:T(8,128)S(1)}, u32[]{:S(2)}, u32[]{:S(2)}) collective-permute-start(f32[256,256]{1,0:T(8,128)S(1)} %shard_map.37), channel_id=1, source_target_pairs={{0,8},{9,1},{18,26},{27,19},{4,20},{13,29},{22,6},{31,15}} | collective-permute-start | bytes 786440 | tf_op jit(solution)/shard_map/ppermute | solution.py:260
  6.2 1.8 %collective-permute-start.1 = (f32[256,256]{1,0:T(8,128)S(1)}, f32[256,256]{1,0:T(8,128)S(1)}, u32[]{:S(2)}, u32[]{:S(2)}) collective-permute-start(f32[256,256]{1,0:T(8,128)S(1)} %shard_map.37), channel_id=1, source_target_pairs={{0,2},{4,6},{9,11},{13,15},{18,16},{22,20},{27,25},{31,29}} | collective-permute-start | bytes 786440 | tf_op jit(solution)/shard_map/ppermute | solution.py:260
  8.0 2.1 %collective-permute-done.3 = f32[256,256]{1,0:T(8,128)S(1)} collective-permute-done((f32[256,256]{1,0:T(8,128)S(1)}, f32[256,256]{1,0:T(8,128)S(1)}, u32[]{:S(2)}, u32[]{:S(2)}) %collective-permute-start.3) | collective-permute-done | bytes 262176 | tf_op jit(solution)/shard_map/ppermute | solution.py:260
  10.1 1.3 collective-permute-start.4
  11.4 0.0 copy-done.1
  11.4 0.7 slice_bitcast_fusion
  12.1 1.9 %collective-permute-start = (f32[256,256]{1,0:T(8,128)}, f32[256,256]{1,0:T(8,128)S(1)}, u32[]{:S(2)}, u32[]{:S(2)}) collective-permute-start(f32[256,256]{1,0:T(8,128)} %slice_bitcast_fusion), channel_id=1, source_target_pairs={{4,0},{9,5},{13,9},{18,14},{22,18},{27,23},{31,27},{0,28}} | collective-permute-start | bytes 786440 | tf_op jit(solution)/shard_map/ppermute | solution.py:260
  14.1 0.1 collective-permute-done.1
  14.2 3.9 %collective-permute-start.2 = (f32[256,256]{1,0:T(8,128)S(1)}, f32[256,256]{1,0:T(8,128)}, u32[]{:S(2)}, u32[]{:S(2)}) collective-permute-start(f32[256,256]{1,0:T(8,128)S(1)} %add.18.refs_4_), channel_id=1, source_target_pairs={{0,1},{2,3},{4,5},{6,7},{9,8},{11,10},{13,12},{15,14},{18,19},{16,... | collective-permute-start | bytes 786440 | tf_op jit(solution)/shard_map/ppermute | solution.py:260
  18.1 0.0 collective-permute-done.4
  18.1 0.1 collective-permute-start.5
  18.2 0.0 copy-done.2
  18.2 0.1 copy.8.refs_0_
  18.3 0.0 collective-permute-done.refs_3_
  18.3 3.6 %collective-permute-done.2.refs_5_ = f32[256,256]{1,0:T(8,128)} collective-permute-done((f32[256,256]{1,0:T(8,128)S(1)}, f32[256,256]{1,0:T(8,128)}, u32[]{:S(2)}, u32[]{:S(2)}) %collective-permute-start.2) | collective-permute-done | bytes 262176 | tf_op jit(solution)/shard_map/ppermute | solution.py:260
  21.9 0.0 collective-permute-done.5.refs_7_
  21.9 0.0 copy-done
  21.9 45.5 %shard_map.38 = (bf16[3,6,256,256]{3,2,1,0:T(8,128)(2,1)S(1)}, f32[256,256]{1,0:T(8,128)S(1)}, f32[256,256]{1,0:T(8,128)S(1)}) custom-call(s32[2,8,2]{2,1,0:T(8,128)S(1)} %copy.8.refs_0_, f32[512,1024]{1,0:T(8,128)S(1)} %copy-done, f32[2,256,256]{2,1,0:T(8,128)S(1)} %copy-done.1, f32[256,256]{1,0:T(8,128)S(1)} %collective-permute-done.refs_3_, ...), custom_call_target="tpu_custom_call" | custom-call | tf_op jit(solution)/shard_map/pallas_call | solution.py:330
  67.5 4.6 %collective-permute-start.10 = (f32[256,256]{1,0:T(8,128)S(1)}, f32[256,256]{1,0:T(8,128)S(1)}, u32[]{:S(2)}, u32[]{:S(2)}) collective-permute-start(f32[256,256]{1,0:T(8,128)S(1)} %get-tuple-element.26), channel_id=1, source_target_pairs={{0,8},{9,1},{18,26},{27,19},{28,12},{5,21},{14,30},{23,7}} | collective-permute-start | bytes 786440 | tf_op jit(solution)/shard_map/ppermute | solution.py:260
  72.1 0.7 collective-permute-start.8
  72.8 3.2 %collective-permute-done.10 = f32[256,256]{1,0:T(8,128)S(1)} collective-permute-done((f32[256,256]{1,0:T(8,128)S(1)}, f32[256,256]{1,0:T(8,128)S(1)}, u32[]{:S(2)}, u32[]{:S(2)}) %collective-permute-start.10) | collective-permute-done | bytes 262176 | tf_op jit(solution)/shard_map/ppermute | solution.py:260
  76.0 1.3 collective-permute-start.11
  77.3 2.8 %shard_map.40 = (f32[256,512]{1,0:T(8,128)S(1)}, f32[256,512]{1,0:T(8,128)S(1)}) custom-call(s32[2,8,2]{2,1,0:T(8,128)S(1)} %copy.8.refs_0_, f32[512,1024]{1,0:T(8,128)S(1)} %copy-done, bf16[3,6,256,256]{3,2,1,0:T(8,128)(2,1)S(1)} %get-tuple-element.20.refs_2_), custom_call_target="tpu_custom_call" | custom-call | tf_op jit(solution)/shard_map/pallas_call | solution.py:330
  80.1 0.1 collective-permute-start.7
  80.2 2.8 %shard_map.39 = (f32[256,256]{1,0:T(8,128)S(1)}, f32[256,256]{1,0:T(8,128)S(1)}, f32[256,256]{1,0:T(8,128)S(1)}, f32[256,256]{1,0:T(8,128)S(1)}) custom-call(s32[2,8,2]{2,1,0:T(8,128)S(1)} %copy.8.refs_0_, f32[512,1024]{1,0:T(8,128)S(1)} %copy-done, bf16[3,6,256,256]{3,2,1,0:T(8,128)(2,1)S(1)} %get-tuple-element.20.refs_2_), custom_call_target="tpu_custom_call" | custom-call | tf_op jit(solution)/shard_map/pallas_call | solution.py:330
  83.0 0.0 collective-permute-done.8
  83.0 1.3 collective-permute-start.9
  84.3 2.5 %collective-permute-done.11 = f32[256,256]{1,0:T(8,128)S(1)} collective-permute-done((f32[256,256]{1,0:T(8,128)S(1)}, f32[256,256]{1,0:T(8,128)S(1)}, u32[]{:S(2)}, u32[]{:S(2)}) %collective-permute-start.11) | collective-permute-done | bytes 262176 | tf_op jit(solution)/shard_map/ppermute | solution.py:260
  86.8 0.2 collective-permute-start.12
  87.0 0.1 collective-permute-start.13
  87.2 1.3 collective-permute-start.14
  88.5 2.8 %collective-permute-done.9.refs_1_ = f32[256,256]{1,0:T(8,128)S(1)} collective-permute-done((f32[256,256]{1,0:T(8,128)S(1)}, f32[256,256]{1,0:T(8,128)S(1)}, u32[]{:S(2)}, u32[]{:S(2)}) %collective-permute-start.9) | collective-permute-done | bytes 262176 | tf_op jit(solution)/shard_map/ppermute | solution.py:260
  91.3 0.8 collective-permute-start.6
  92.0 0.0 collective-permute-done.12.refs_3_
  92.1 39.4 %shard_map.41.refs_5_ = bf16[3,6,256,256]{3,2,1,0:T(8,128)(2,1)S(1)} custom-call(f32[256,256]{1,0:T(8,128)S(1)} %add.21.refs_0_, f32[256,256]{1,0:T(8,128)S(1)} %collective-permute-done.9.refs_1_, f32[256,256]{1,0:T(8,128)S(1)} %add.23.refs_2_, f32[256,256]{1,0:T(8,128)S(1)} %collective-permute-done.12.refs_3_), custom_call_target="tpu_custom_call" | custom-call | tf_op jit(solution)/shard_map/pallas_call | solution.py:330
  131.5 0.0 collective-permute-done.13.refs_3_
  131.5 0.0 collective-permute-done.14.refs_4_
  131.5 0.0 collective-permute-done.7.refs_4_.refs_2_
  131.5 2.8 %shard_map.43 = (f32[256,512]{1,0:T(8,128)S(1)}, f32[256,512]{1,0:T(8,128)S(1)}) custom-call(s32[2,8,2]{2,1,0:T(8,128)S(1)} %copy.8.refs_0_, f32[256,512]{1,0:T(8,128)S(1)} %get-tuple-element.22.refs_2_.refs_1_, f32[256,512]{1,0:T(8,128)S(1)} %collective-permute-done.7.refs_4_.refs_2_, f32[256,256]{1,0:T(8,128)S(1)} %collective-permute-done.13.refs_3_, ...), custom_call_target="tpu_custom_call" | custom-call | tf_op jit(solution)/shard_map/pallas_call | solution.py:330
  134.3 1.6 collective-permute-start.16
  135.9 0.0 collective-permute-done.6.refs_3_
  135.9 2.8 %shard_map.42 = (f32[256,256]{1,0:T(8,128)S(1)}, f32[256,256]{1,0:T(8,128)S(1)}, f32[256,256]{1,0:T(8,128)S(1)}, f32[256,256]{1,0:T(8,128)S(1)}) custom-call(s32[2,8,2]{2,1,0:T(8,128)S(1)} %copy.8.refs_0_, f32[256,256]{1,0:T(8,128)S(1)} %get-tuple-element.21.refs_1_, f32[256,512]{1,0:T(8,128)S(1)} %get-tuple-element.22.refs_2_.refs_1_, ...), custom_call_target="tpu_custom_call" | custom-call | tf_op jit(solution)/shard_map/pallas_call | solution.py:330
  138.7 0.1 collective-permute-start.15
  138.8 2.5 %collective-permute-start.17 = (f32[256,256]{1,0:T(8,128)S(1)}, f32[256,256]{1,0:T(8,128)S(1)}, u32[]{:S(2)}, u32[]{:S(2)}) collective-permute-start(f32[256,256]{1,0:T(8,128)S(1)} %get-tuple-element.33), channel_id=1, source_target_pairs={{0,1},{1,2},{2,3},{3,0},{4,5},{5,6},{6,7},{7,4},{8,9},{9,10},{10,1... | collective-permute-start | bytes 786440 | tf_op jit(solution)/shard_map/ppermute | solution.py:312
  141.3 0.0 collective-permute-start.18
  141.3 0.9 shard_map.44.partial
  142.2 14.1 %collective-permute-done.15.last_in = f32[256,256]{1,0:T(8,128)S(1)} collective-permute-done((f32[256,256]{1,0:T(8,128)S(1)}, f32[256,256]{1,0:T(8,128)S(1)}, u32[]{:S(2)}, u32[]{:S(2)}) %collective-permute-start.15) | collective-permute-done | bytes 262176 | tf_op jit(solution)/shard_map/ppermute | solution.py:308
  156.3 0.0 collective-permute-done.17.col_in
  156.3 7.8 %collective-permute-done.18.corner_in = f32[256,256]{1,0:T(8,128)S(1)} collective-permute-done((f32[256,256]{1,0:T(8,128)S(1)}, f32[256,256]{1,0:T(8,128)S(1)}, u32[]{:S(2)}, u32[]{:S(2)}) %collective-permute-start.18) | collective-permute-done | bytes 262176 | tf_op jit(solution)/shard_map/ppermute | solution.py:260
  164.1 0.0 collective-permute-done.16.others_in
  164.1 1.1 shard_map.45
  (6 shorter events, 0.2 us)
Async XLA Ops:
  0.0 11.4 %copy-start.1 = (f32[2,256,256]{2,1,0:T(8,128)S(1)}, f32[2,256,256]{2,1,0:T(8,128)}, u32[]{:S(2)}) copy-start(f32[2,256,256]{2,1,0:T(8,128)} %refs_2_.1) | copy-start | bytes 1572868
  1.2 17.0 %copy-start.2 = (s32[2,8,2]{1,2,0:T(2,128)S(1)}, s32[2,8,2]{1,2,0:T(2,128)}, u32[]{:S(2)}) copy-start(s32[2,8,2]{1,2,0:T(2,128)} %param.5) | copy-start | bytes 388
  1.2 20.8 %copy-start = (f32[512,1024]{1,0:T(8,128)S(1)}, f32[512,1024]{1,0:T(8,128)}, u32[]{:S(2)}) copy-start(f32[512,1024]{1,0:T(8,128)} %refs_1_.5) | copy-start | bytes 6291460
  1.2 8.9 %collective-permute-start.3 = (f32[256,256]{1,0:T(8,128)S(1)}, f32[256,256]{1,0:T(8,128)S(1)}, u32[]{:S(2)}, u32[]{:S(2)}) collective-permute-start(f32[256,256]{1,0:T(8,128)S(1)} %shard_map.37), channel_id=1, source_target_pairs={{0,8},{9,1},{18,26},{27,19},{4,20},{13,29},{22,6},{31,15}} | collective-permute-start | bytes 786440 | tf_op jit(solution)/shard_map/ppermute | solution.py:260
  6.2 7.9 %collective-permute-start.1 = (f32[256,256]{1,0:T(8,128)S(1)}, f32[256,256]{1,0:T(8,128)S(1)}, u32[]{:S(2)}, u32[]{:S(2)}) collective-permute-start(f32[256,256]{1,0:T(8,128)S(1)} %shard_map.37), channel_id=1, source_target_pairs={{0,2},{4,6},{9,11},{13,15},{18,16},{22,20},{27,25},{31,29}} | collective-permute-start | bytes 786440 | tf_op jit(solution)/shard_map/ppermute | solution.py:260
  10.1 8.0 %collective-permute-start.4 = (f32[256,256]{1,0:T(8,128)S(1)}, f32[256,256]{1,0:T(8,128)S(1)}, u32[]{:S(2)}, u32[]{:S(2)}) collective-permute-start(f32[256,256]{1,0:T(8,128)S(1)} %add.19), channel_id=1, source_target_pairs={{0,16},{8,24},{9,25},{1,17},{18,2},{26,10},{27,11},{19,3},{4,12},{... | collective-permute-start | bytes 786440 | tf_op jit(solution)/shard_map/ppermute | solution.py:260
  12.1 6.1 %collective-permute-start = (f32[256,256]{1,0:T(8,128)}, f32[256,256]{1,0:T(8,128)S(1)}, u32[]{:S(2)}, u32[]{:S(2)}) collective-permute-start(f32[256,256]{1,0:T(8,128)} %slice_bitcast_fusion), channel_id=1, source_target_pairs={{4,0},{9,5},{13,9},{18,14},{22,18},{27,23},{31,27},{0,28}} | collective-permute-start | bytes 786440 | tf_op jit(solution)/shard_map/ppermute | solution.py:260
  14.2 7.7 %collective-permute-start.2 = (f32[256,256]{1,0:T(8,128)S(1)}, f32[256,256]{1,0:T(8,128)}, u32[]{:S(2)}, u32[]{:S(2)}) collective-permute-start(f32[256,256]{1,0:T(8,128)S(1)} %add.18.refs_4_), channel_id=1, source_target_pairs={{0,1},{2,3},{4,5},{6,7},{9,8},{11,10},{13,12},{15,14},{18,19},{16,... | collective-permute-start | bytes 786440 | tf_op jit(solution)/shard_map/ppermute | solution.py:260
  18.1 3.8 %collective-permute-start.5 = (f32[256,256]{1,0:T(8,128)S(1)}, f32[256,256]{1,0:T(8,128)}, u32[]{:S(2)}, u32[]{:S(2)}) collective-permute-start(f32[256,256]{1,0:T(8,128)S(1)} %add.20.refs_6_), channel_id=1, source_target_pairs={{0,4},{4,0},{8,12},{12,8},{16,20},{20,16},{24,28},{28,24},{1,5},{5... | collective-permute-start | bytes 786440 | tf_op jit(solution)/shard_map/ppermute | solution.py:300
  67.5 8.5 %collective-permute-start.10 = (f32[256,256]{1,0:T(8,128)S(1)}, f32[256,256]{1,0:T(8,128)S(1)}, u32[]{:S(2)}, u32[]{:S(2)}) collective-permute-start(f32[256,256]{1,0:T(8,128)S(1)} %get-tuple-element.26), channel_id=1, source_target_pairs={{0,8},{9,1},{18,26},{27,19},{28,12},{5,21},{14,30},{23,7}} | collective-permute-start | bytes 786440 | tf_op jit(solution)/shard_map/ppermute | solution.py:260
  72.1 10.9 %collective-permute-start.8 = (f32[256,256]{1,0:T(8,128)S(1)}, f32[256,256]{1,0:T(8,128)S(1)}, u32[]{:S(2)}, u32[]{:S(2)}) collective-permute-start(f32[256,256]{1,0:T(8,128)S(1)} %get-tuple-element.25), channel_id=1, source_target_pairs={{3,1},{4,6},{8,10},{13,15},{17,19},{22,20},{26,24},{31,29}} | collective-permute-start | bytes 786440 | tf_op jit(solution)/shard_map/ppermute | solution.py:260
  76.0 10.8 %collective-permute-start.11 = (f32[256,256]{1,0:T(8,128)S(1)}, f32[256,256]{1,0:T(8,128)S(1)}, u32[]{:S(2)}, u32[]{:S(2)}) collective-permute-start(f32[256,256]{1,0:T(8,128)S(1)} %add.22), channel_id=1, source_target_pairs={{0,16},{8,24},{9,25},{1,17},{18,2},{26,10},{27,11},{19,3},{28,20},... | collective-permute-start | bytes 786440 | tf_op jit(solution)/shard_map/ppermute | solution.py:260
  80.1 51.4 %collective-permute-start.7 = (f32[256,512]{1,0:T(8,128)S(1)}, f32[256,512]{1,0:T(8,128)S(1)}, u32[]{:S(2)}, u32[]{:S(2)}) collective-permute-start(f32[256,512]{1,0:T(8,128)S(1)} %get-tuple-element.24), channel_id=1, source_target_pairs={{0,4},{4,8},{8,12},{12,16},{16,20},{20,24},{24,28},{28,0},{1,5},{5... | collective-permute-start | bytes 1572872 | tf_op jit(solution)/shard_map/ppermute | solution.py:308
  83.0 8.3 %collective-permute-start.9 = (f32[256,256]{1,0:T(8,128)S(1)}, f32[256,256]{1,0:T(8,128)S(1)}, u32[]{:S(2)}, u32[]{:S(2)}) collective-permute-start(f32[256,256]{1,0:T(8,128)S(1)} %add.21.refs_0_), channel_id=1, source_target_pairs={{3,2},{1,0},{4,5},{6,7},{8,9},{10,11},{13,12},{15,14},{17,16},{19,... | collective-permute-start | bytes 786440 | tf_op jit(solution)/shard_map/ppermute | solution.py:260
  86.8 5.2 %collective-permute-start.12 = (f32[256,256]{1,0:T(8,128)S(1)}, f32[256,256]{1,0:T(8,128)S(1)}, u32[]{:S(2)}, u32[]{:S(2)}) collective-permute-start(f32[256,256]{1,0:T(8,128)S(1)} %add.23.refs_2_), channel_id=1, source_target_pairs={{0,4},{4,0},{8,12},{12,8},{16,20},{20,16},{24,28},{28,24},{1,5},{5... | collective-permute-start | bytes 786440 | tf_op jit(solution)/shard_map/ppermute | solution.py:300
  87.0 44.4 %collective-permute-start.13 = (f32[256,256]{1,0:T(8,128)S(1)}, f32[256,256]{1,0:T(8,128)S(1)}, u32[]{:S(2)}, u32[]{:S(2)}) collective-permute-start(f32[256,256]{1,0:T(8,128)S(1)} %get-tuple-element.28), channel_id=1, source_target_pairs={{0,1},{1,2},{2,3},{3,0},{4,5},{5,6},{6,7},{7,4},{8,9},{9,10},{10,1... | collective-permute-start | bytes 786440 | tf_op jit(solution)/shard_map/ppermute | solution.py:312
  87.2 44.3 %collective-permute-start.14 = (f32[256,256]{1,0:T(8,128)S(1)}, f32[256,256]{1,0:T(8,128)S(1)}, u32[]{:S(2)}, u32[]{:S(2)}) collective-permute-start(f32[256,256]{1,0:T(8,128)S(1)} %get-tuple-element.29), channel_id=1, source_target_pairs={{0,5},{1,6},{2,7},{3,4},{4,9},{5,10},{6,11},{7,8},{8,13},{9,14},{1... | collective-permute-start | bytes 786440 | tf_op jit(solution)/shard_map/ppermute | solution.py:260
  91.3 44.6 %collective-permute-start.6 = (f32[256,256]{1,0:T(8,128)S(1)}, f32[256,256]{1,0:T(8,128)S(1)}, u32[]{:S(2)}, u32[]{:S(2)}) collective-permute-start(f32[256,256]{1,0:T(8,128)S(1)} %get-tuple-element.23), channel_id=1, source_target_pairs={{0,4},{4,8},{8,12},{12,16},{16,20},{20,24},{24,28},{28,0},{1,5},{5... | collective-permute-start | bytes 786440 | tf_op jit(solution)/shard_map/ppermute | solution.py:308
  134.3 29.8 %collective-permute-start.16 = (f32[256,512]{1,0:T(8,128)S(1)}, f32[256,512]{1,0:T(8,128)S(1)}, u32[]{:S(2)}, u32[]{:S(2)}) collective-permute-start(f32[256,512]{1,0:T(8,128)S(1)} %get-tuple-element.32), channel_id=1, source_target_pairs={{0,4},{4,8},{8,12},{12,16},{16,20},{20,24},{24,28},{28,0},{1,5},{5... | collective-permute-start | bytes 1572872 | tf_op jit(solution)/shard_map/ppermute | solution.py:308
  138.7 17.6 %collective-permute-start.15 = (f32[256,256]{1,0:T(8,128)S(1)}, f32[256,256]{1,0:T(8,128)S(1)}, u32[]{:S(2)}, u32[]{:S(2)}) collective-permute-start(f32[256,256]{1,0:T(8,128)S(1)} %get-tuple-element.31), channel_id=1, source_target_pairs={{0,4},{4,8},{8,12},{12,16},{16,20},{20,24},{24,28},{28,0},{1,5},{5... | collective-permute-start | bytes 786440 | tf_op jit(solution)/shard_map/ppermute | solution.py:308
  138.8 17.5 %collective-permute-start.17 = (f32[256,256]{1,0:T(8,128)S(1)}, f32[256,256]{1,0:T(8,128)S(1)}, u32[]{:S(2)}, u32[]{:S(2)}) collective-permute-start(f32[256,256]{1,0:T(8,128)S(1)} %get-tuple-element.33), channel_id=1, source_target_pairs={{0,1},{1,2},{2,3},{3,0},{4,5},{5,6},{6,7},{7,4},{8,9},{9,10},{10,1... | collective-permute-start | bytes 786440 | tf_op jit(solution)/shard_map/ppermute | solution.py:312
  141.3 22.8 %collective-permute-start.18 = (f32[256,256]{1,0:T(8,128)S(1)}, f32[256,256]{1,0:T(8,128)S(1)}, u32[]{:S(2)}, u32[]{:S(2)}) collective-permute-start(f32[256,256]{1,0:T(8,128)S(1)} %get-tuple-element.34), channel_id=1, source_target_pairs={{0,5},{1,6},{2,7},{3,4},{4,9},{5,10},{6,11},{7,8},{8,13},{9,14},{1... | collective-permute-start | bytes 786440 | tf_op jit(solution)/shard_map/ppermute | solution.py:260

commit v2 on v1

--- a/solution.py
+++ b/solution.py
@@ -149,38 +149,52 @@
     out[...] = jnp.where(group == col, coupling[...] / (2.0 * gap[...]), 0.0)
 
 
-def find_factors(shape, carried, parts, factor_out, generators, weights):
+def write_factors(generators, weights, targets):
+    for index, (target, place) in enumerate(targets):
+        plain = generators[index]
+        for part, value in enumerate((plain, plain.T, weights[index])):
+            target[place, 2 * part], target[place, 2 * part + 1] = split(value)
+
+
+def order_band(shape, carried, band_parts, generators, first):
     band_pairs = shape[0] // shape[1]
     lane = places(shape)[3]
-    generators[0] = parts[0][...] + parts[1][...]
-    for shift, part in enumerate(parts[2:]):
-        generators[1 + lax.rem(lane + carried - shift + band_pairs, band_pairs)] = part[...]
+    for shift, part in enumerate(band_parts):
+        generators[first + lax.rem(lane + carried - shift + band_pairs, band_pairs)] = part[...]
+
+
+def band_weights_kernel(shape, carried, *refs):
+    band_parts, (band_out, generators, weights) = refs[:-3], refs[-3:]
+    order_band(shape, carried, band_parts, generators, 0)
     invert(generators, weights)
-    for index in range(1 + band_pairs):
-        plain = generators[index]
-        for part, value in enumerate((plain, plain.T, weights[index])):
-            factor_out[index, 2 * part], factor_out[index, 2 * part + 1] = split(value)
+    write_factors(generators, weights, [(band_out, pair) for pair in range(len(band_parts))])
 
 
 def weights_kernel(shape, carried, *refs):
-    find_factors(shape, carried, refs[:-3], *refs[-3:])
-
-
-def weights_and_next_kernel(shape, step, carried, *refs):
-    rows, cols = shape
-    band_pairs = rows // cols
-    orders, matrix, own_gap, next_gap = refs[:4]
-    factor_out, row_out, band_out, generators, weights = refs[6 + band_pairs :]
+    row_parts, band_parts, (row_out, band_out, generators, weights) = refs[:2], refs[2:-4], refs[-4:]
+    generators[0] = row_parts[0][...] + row_parts[1][...]
+    order_band(shape, carried, band_parts, generators, 1)
+    invert(generators, weights)
+    write_factors(generators, weights, [(row_out, 0)] + [(band_out, pair) for pair in range(len(band_parts))])
+
+
+def row_weights_and_next_kernel(shape, step, *refs):
+    rows, cols = shape
+    band_pairs = rows // cols
+    orders, matrix, own_gap, next_gap, band_in, first_part, second_part = refs[:7]
+    row_factors, row_out, band_out, generators, weights = refs[7:]
     width = row_out.shape[0]
     row, col, _, _ = places(shape)
     before, after = lax.rem(row - 1 + rows, rows), lax.rem(row + 1, rows)
-    find_factors(shape, carried, refs[4 : 6 + band_pairs], factor_out, generators, weights)
+    generators[0] = first_part[...] + second_part[...]
+    invert(generators, weights)
+    write_factors(generators, weights, [(row_factors, 0)])
 
     def coupling(pair, row_flag, col_flag):
         cols = pl.ds(pl.multiple_of(pair * (2 * width), 2 * width), 2 * width)
-        top, bottom = turn_rows(matrix[:width, cols], matrix[width:, cols], factors(factor_out, 0))
+        top, bottom = turn_rows(matrix[:width, cols], matrix[width:, cols], factors(row_factors, 0))
         picked = jnp.where(row_flag == 0, top, bottom)
-        left, right = turn_columns(picked[:, :width], picked[:, width:], factors(factor_out, 1 + pair))
+        left, right = turn_columns(picked[:, :width], picked[:, width:], factors(band_in, pair))
         return jnp.where(col_flag == 0, left, right)
 
     row_here, band_here = lax.div(before, band_pairs) == col, lax.div(after, band_pairs) == col
@@ -206,17 +220,17 @@
 
 def rotate_kernel(shape, step, pairs, quarters, *refs):
     count = 1 + max(quarter[0] for corners in quarters for quarter in corners)
-    orders, factor_in, outputs = refs[0], refs[1 + count], refs[2 + count :]
+    orders, row_factors, factor_in, outputs = refs[0], refs[1 + count], refs[2 + count], refs[3 + count :]
     band_pairs = shape[0] // shape[1]
     width = factor_in.shape[2]
     row, col, _, _ = places(shape)
-    own = factors(factor_in, 0)
+    own = factors(row_factors, 0)
     keep_rows = orders[step, row, 0] == 0
     for index, (pair, corners) in enumerate(zip(pairs, quarters)):
         tiles = [refs[1 + which][pl.ds(at_row, width), pl.ds(at_col, width)] for which, at_row, at_col in corners]
         first, second = jnp.concatenate(tiles[:2], axis=1), jnp.concatenate(tiles[2:], axis=1)
         top, bottom = turn_rows(first, second, own)
-        parts = factors(factor_in, 1 + pair)
+        parts = factors(factor_in, pair)
         keep_cols = orders[step, col * band_pairs + pair, 0] == 0
         first = jnp.concatenate([top[:, :width], bottom[:, :width]], axis=0)
         second = jnp.concatenate([top[:, width:], bottom[:, width:]], axis=0)
@@ -381,7 +395,7 @@
     square = pltpu.VMEM((width, width), F32)
     many = pltpu.VMEM((width, wide - 2 * width), F32)
     stack = pltpu.VMEM((1 + band_pairs, width, width), F32)
-    split_stack = pltpu.VMEM((1 + band_pairs, 6, width, width), BF16)
+    row_stack, band_stack = (pltpu.VMEM((count, 6, width, width), BF16) for count in (1, band_pairs))
     dma = pltpu.SemaphoreType.DMA
 
     row_value = call(
@@ -398,7 +412,9 @@
         carried = int(step > 0)
         parts = spread(row_value, band_value, shape, carried)
         if step == steps - 1:
-            split_factors = call(functools.partial(weights_kernel, shape, carried), split_stack, parts, [stack, stack])
+            split_factors = call(
+                functools.partial(weights_kernel, shape, carried), (row_stack, band_stack), parts, [stack, stack]
+            )
         else:
             if step > 0:
                 matrix = finish(pieces, width, tall, wide)
@@ -407,13 +423,20 @@
                 for row in range(rows)
             ]
             next_gap = send(gap_table[step + 1], wanted)
-            split_factors, row_value, band_value = call(
-                functools.partial(weights_and_next_kernel, shape, step, carried),
-                (split_stack, square, square),
-                (orders, matrix, gap_table, next_gap, *parts),
-                [stack, stack],
+            band_factors = call(
+                functools.partial(band_weights_kernel, shape, carried),
+                band_stack,
+                parts[2:],
+                [pltpu.VMEM((band_pairs, width, width), F32)] * 2,
+            )
+            row_factors, row_value, band_value = call(
+                functools.partial(row_weights_and_next_kernel, shape, step),
+                (row_stack, square, square),
+                (orders, matrix, gap_table, next_gap, band_factors, *parts[:2]),
+                [pltpu.VMEM((1, width, width), F32)] * 2,
                 specs={0: SMEM},
             )
+            split_factors = (row_factors, band_factors)
         if step < steps - 1 or steps == 1:
             tiles = lambda pair: tuple((0, i * width, (2 * pair + j) * width) for i in (0, 1) for j in (0, 1))
             last_inputs, last_tiles = (matrix,), (tiles(last_pair),)
@@ -435,13 +458,13 @@
         last_stay, last_leave, col_piece, corner_piece = call(
             functools.partial(rotate_kernel, shape, step, (last_pair,), last_tiles),
             (square,) * 4,
-            (orders, *last_inputs, split_factors),
+            (orders, *last_inputs, *split_factors),
             specs={0: SMEM},
         )
         others, others_leave = call(
             functools.partial(rotate_kernel, shape, step, tuple(range(last_pair)), other_tiles),
             (many, many),
-            (orders, *other_inputs, split_factors),
+            (orders, *other_inputs, *split_factors),
             specs={0: SMEM},
         )
         col_in = to_next_cols(col_piece, shape)

time: 166 us -> 155 us (0.934)
  waiting for transfers between devices: 36.1 us -> 26.6 us
  starting transfers between devices: 28.5 us -> 25.5 us
  Pallas kernels: 99.3 us -> 101 us
    ppermute x4, waiting for transfers between devices: 14.1 us -> 3.9 us  [to_next_rows(): lax.ppermute(value, 'rows', [(r, (r + 1) % shape[0]) for r in range(shape...]
    ppermute x11, starting transfers between devices: 23.1 us -> 17.3 us  [send(): return lax.ppermute(value, ('rows', 'cols'), pairs)]
    ppermute x2, waiting for transfers between devices: 0.01 us -> 3.68 us  [to_next_cols(): lax.ppermute(value, 'cols', [(c, (c + 1) % shape[1]) for c in range(shape...]
    ppermute x11, waiting for transfers between devices: 22 us -> 19 us  [send(): return lax.ppermute(value, ('rows', 'cols'), pairs)]
    ppermute x2, starting transfers between devices: 0.3 us -> 2.36 us  [within_group(): lax.ppermute(value, 'rows', [(row, row // band_pairs * band_pairs + (row...]
    pallas_call x9 -> x10, Pallas kernels: 99.3 us -> 101 us  [call(): pl.pallas_call(kernel, out_shape=outputs, in_specs=[specs.get(index, VMEM...]
  transfers between devices with their start and end apart: 19 -> 19, of which waited for: 8 -> 7; matrix products, arithmetic and copies ran while one was open for 1% -> 1% of each run, Pallas kernels for 31% -> 53%
where the time goes in v2:
time: 155 us; the launch traced here: 154 us
  Pallas kernels  101 us (65%)
  waiting for transfers between devices  26.6 us (17%)
  starting transfers between devices  25.5 us (16%)
    pallas_call x10, Pallas kernels, call(): pl.pallas_call(kernel, out_shape=outputs, in_specs=[specs.get(index, VMEM...  101 us
    ppermute x11, waiting for transfers between devices, send(): return lax.ppermute(value, ('rows', 'cols'), pairs)  19 us
    ppermute x11, starting transfers between devices, send(): return lax.ppermute(value, ('rows', 'cols'), pairs)  17.3 us
    ppermute x4, waiting for transfers between devices, to_next_rows(): lax.ppermute(value, 'rows', [(r, (r + 1) % shape[0]) for r in range(shape...  3.9 us
    ppermute x2, waiting for transfers between devices, to_next_cols(): lax.ppermute(value, 'cols', [(c, (c + 1) % shape[1]) for c in range(shape...  3.68 us
  transfers between devices with their start and end apart: 19, of which 7 were waited for; matrix products, arithmetic and copies ran while one was open for 1% of the time, Pallas kernels for 53%

profile of v2, /device:TPU:0, one launch (start us, length us, event | category | flops | bytes accessed | tf_op | source)
XLA Modules:
  0.0 154.2 jit_solution(8595503068117665351)
XLA Ops:
  0.0 0.0 copy-start.1
  0.0 1.1 shard_map.37
  1.2 0.0 copy-start.2
  1.2 4.9 %collective-permute-start.1 = (f32[256,256]{1,0:T(8,128)S(1)}, f32[256,256]{1,0:T(8,128)S(1)}, u32[]{:S(2)}, u32[]{:S(2)}) collective-permute-start(f32[256,256]{1,0:T(8,128)S(1)} %shard_map.37), channel_id=1, source_target_pairs={{0,8},{9,1},{18,26},{27,19},{4,20},{13,29},{22,6},{31,15}} | collective-permute-start | bytes 786440 | tf_op jit(solution)/shard_map/ppermute | solution.py:274
  6.1 3.9 %collective-permute-done.1 = f32[256,256]{1,0:T(8,128)S(1)} collective-permute-done((f32[256,256]{1,0:T(8,128)S(1)}, f32[256,256]{1,0:T(8,128)S(1)}, u32[]{:S(2)}, u32[]{:S(2)}) %collective-permute-start.1) | collective-permute-done | bytes 262176 | tf_op jit(solution)/shard_map/ppermute | solution.py:274
  10.0 0.0 copy-start
  10.0 1.4 collective-permute-start.2
  11.4 1.3 collective-permute-start.4
  12.7 0.0 copy-done.1
  12.7 0.7 slice_bitcast_fusion
  13.5 1.9 %collective-permute-start = (f32[256,256]{1,0:T(8,128)}, f32[256,256]{1,0:T(8,128)S(1)}, u32[]{:S(2)}, u32[]{:S(2)}) collective-permute-start(f32[256,256]{1,0:T(8,128)} %slice_bitcast_fusion), channel_id=1, source_target_pairs={{4,0},{9,5},{13,9},{18,14},{22,18},{27,23},{31,27},{0,28}} | collective-permute-start | bytes 786440 | tf_op jit(solution)/shard_map/ppermute | solution.py:274
  15.4 0.0 collective-permute-done.2
  15.4 2.0 %collective-permute-start.3 = (f32[256,256]{1,0:T(8,128)S(1)}, f32[256,256]{1,0:T(8,128)}, u32[]{:S(2)}, u32[]{:S(2)}) collective-permute-start(f32[256,256]{1,0:T(8,128)S(1)} %add.19.refs_0_), channel_id=1, source_target_pairs={{0,4},{4,0},{8,12},{12,8},{16,20},{20,16},{24,28},{28,24},{1,5},{5... | collective-permute-start | bytes 786440 | tf_op jit(solution)/shard_map/ppermute | solution.py:314
  17.5 0.0 collective-permute-done.4
  17.5 3.1 %collective-permute-start.5 = (f32[256,256]{1,0:T(8,128)S(1)}, f32[256,256]{1,0:T(8,128)}, u32[]{:S(2)}, u32[]{:S(2)}) collective-permute-start(f32[256,256]{1,0:T(8,128)S(1)} %add.20.refs_5_), channel_id=1, source_target_pairs={{0,1},{2,3},{4,5},{6,7},{9,8},{11,10},{13,12},{15,14},{18,19},{16,... | collective-permute-start | bytes 786440 | tf_op jit(solution)/shard_map/ppermute | solution.py:274
  20.6 0.0 copy-done.2
  20.6 0.1 copy.8.refs_0_
  20.7 0.0 collective-permute-done.3.refs_1_
  20.7 29.6 %shard_map.38.refs_4_.refs_3_ = bf16[2,6,256,256]{3,2,1,0:T(8,128)(2,1)S(1)} custom-call(f32[256,256]{1,0:T(8,128)S(1)} %add.19.refs_0_, f32[256,256]{1,0:T(8,128)} %collective-permute-done.3.refs_1_), custom_call_target="tpu_custom_call" | custom-call | tf_op jit(solution)/shard_map/pallas_call | solution.py:344
  50.4 0.0 collective-permute-done.refs_3_
  50.4 0.0 collective-permute-done.5.refs_6_
  50.4 0.0 copy-done
  50.4 17.3 %shard_map.39 = (bf16[1,6,256,256]{3,2,1,0:T(8,128)(2,1)S(1)}, f32[256,256]{1,0:T(8,128)S(1)}, f32[256,256]{1,0:T(8,128)S(1)}) custom-call(s32[2,8,2]{2,1,0:T(8,128)S(1)} %copy.8.refs_0_, f32[512,1024]{1,0:T(8,128)S(1)} %copy-done, f32[2,256,256]{2,1,0:T(8,128)S(1)} %copy-done.1, f32[256,256]{1,0:T(8,128)S(1)} %collective-permute-done.refs_3_, ...), custom_call_target="tpu_custom_call" | custom-call | tf_op jit(solution)/shard_map/pallas_call | solution.py:344
  67.7 1.3 collective-permute-start.10
  69.0 0.7 collective-permute-start.8
  69.7 3.2 %collective-permute-done.10 = f32[256,256]{1,0:T(8,128)S(1)} collective-permute-done((f32[256,256]{1,0:T(8,128)S(1)}, f32[256,256]{1,0:T(8,128)S(1)}, u32[]{:S(2)}, u32[]{:S(2)}) %collective-permute-start.10) | collective-permute-done | bytes 262176 | tf_op jit(solution)/shard_map/ppermute | solution.py:274
  72.9 1.3 collective-permute-start.11
  74.3 2.8 %shard_map.41 = (f32[256,512]{1,0:T(8,128)S(1)}, f32[256,512]{1,0:T(8,128)S(1)}) custom-call(s32[2,8,2]{2,1,0:T(8,128)S(1)} %copy.8.refs_0_, f32[512,1024]{1,0:T(8,128)S(1)} %copy-done, bf16[1,6,256,256]{3,2,1,0:T(8,128)(2,1)S(1)} %get-tuple-element.22.refs_2_, bf16[2,6,256,256]{3,2,1,0:T(8,128)(2,1)S(1)} %shard_map.38.refs_4_.refs_3_), custom_call_target="tpu_custom_call" | custom-call | tf_op jit(solution)/shard_map/pallas_call | solution.py:344
  77.0 0.2 collective-permute-start.7
  77.3 2.8 %shard_map.40 = (f32[256,256]{1,0:T(8,128)S(1)}, f32[256,256]{1,0:T(8,128)S(1)}, f32[256,256]{1,0:T(8,128)S(1)}, f32[256,256]{1,0:T(8,128)S(1)}) custom-call(s32[2,8,2]{2,1,0:T(8,128)S(1)} %copy.8.refs_0_, f32[512,1024]{1,0:T(8,128)S(1)} %copy-done, bf16[1,6,256,256]{3,2,1,0:T(8,128)(2,1)S(1)} %get-tuple-element.22.refs_2_, ...), custom_call_target="tpu_custom_call" | custom-call | tf_op jit(solution)/shard_map/pallas_call | solution.py:344
  80.0 0.0 collective-permute-done.8
  80.1 1.3 collective-permute-start.9
  81.4 2.4 %collective-permute-done.11 = f32[256,256]{1,0:T(8,128)S(1)} collective-permute-done((f32[256,256]{1,0:T(8,128)S(1)}, f32[256,256]{1,0:T(8,128)S(1)}, u32[]{:S(2)}, u32[]{:S(2)}) %collective-permute-start.11) | collective-permute-done | bytes 262176 | tf_op jit(solution)/shard_map/ppermute | solution.py:274
  83.8 0.3 collective-permute-start.12
  84.1 0.6 collective-permute-start.13
  84.7 0.1 collective-permute-start.14
  84.7 3.6 %collective-permute-done.9.refs_1_ = f32[256,256]{1,0:T(8,128)S(1)} collective-permute-done((f32[256,256]{1,0:T(8,128)S(1)}, f32[256,256]{1,0:T(8,128)S(1)}, u32[]{:S(2)}, u32[]{:S(2)}) %collective-permute-start.9) | collective-permute-done | bytes 262176 | tf_op jit(solution)/shard_map/ppermute | solution.py:274
  88.4 0.3 collective-permute-start.6
  88.7 0.0 collective-permute-done.12.refs_3_
  88.7 39.4 %shard_map.42 = (bf16[1,6,256,256]{3,2,1,0:T(8,128)(2,1)S(1)}, bf16[2,6,256,256]{3,2,1,0:T(8,128)(2,1)S(1)}) custom-call(f32[256,256]{1,0:T(8,128)S(1)} %add.21.refs_0_, f32[256,256]{1,0:T(8,128)S(1)} %collective-permute-done.9.refs_1_, f32[256,256]{1,0:T(8,128)S(1)} %add.23.refs_2_, f32[256,256]{1,0:T(8,128)S(1)} %collective-permute-done.12.refs_3_), custom_call_target="tpu_custom_call" | custom-call | tf_op jit(solution)/shard_map/pallas_call | solution.py:344
  128.1 0.0 collective-permute-done.13.refs_3_
  128.1 0.0 collective-permute-done.14.refs_4_
  128.1 0.0 collective-permute-done.7.refs_4_.refs_2_
  128.1 2.8 %shard_map.44 = (f32[256,512]{1,0:T(8,128)S(1)}, f32[256,512]{1,0:T(8,128)S(1)}) custom-call(s32[2,8,2]{2,1,0:T(8,128)S(1)} %copy.8.refs_0_, f32[256,512]{1,0:T(8,128)S(1)} %get-tuple-element.24.refs_2_.refs_1_, f32[256,512]{1,0:T(8,128)S(1)} %collective-permute-done.7.refs_4_.refs_2_, f32[256,256]{1,0:T(8,128)S(1)} %collective-permute-done.13.refs_3_, ...), custom_call_target="tpu_custom_call" | custom-call | tf_op jit(solution)/shard_map/pallas_call | solution.py:344
  130.9 2.1 %collective-permute-start.16 = (f32[256,512]{1,0:T(8,128)S(1)}, f32[256,512]{1,0:T(8,128)S(1)}, u32[]{:S(2)}, u32[]{:S(2)}) collective-permute-start(f32[256,512]{1,0:T(8,128)S(1)} %get-tuple-element.36), channel_id=1, source_target_pairs={{0,4},{4,8},{8,12},{12,16},{16,20},{20,24},{24,28},{28,0},{1,5},{5... | collective-permute-start | bytes 1572872 | tf_op jit(solution)/shard_map/ppermute | solution.py:322
  133.1 0.0 collective-permute-done.6.refs_3_
  133.1 2.8 %shard_map.43 = (f32[256,256]{1,0:T(8,128)S(1)}, f32[256,256]{1,0:T(8,128)S(1)}, f32[256,256]{1,0:T(8,128)S(1)}, f32[256,256]{1,0:T(8,128)S(1)}) custom-call(s32[2,8,2]{2,1,0:T(8,128)S(1)} %copy.8.refs_0_, f32[256,256]{1,0:T(8,128)S(1)} %get-tuple-element.23.refs_1_, f32[256,512]{1,0:T(8,128)S(1)} %get-tuple-element.24.refs_2_.refs_1_, ...), custom_call_target="tpu_custom_call" | custom-call | tf_op jit(solution)/shard_map/pallas_call | solution.py:344
  135.9 0.1 collective-permute-start.15
  135.9 2.5 %collective-permute-start.17 = (f32[256,256]{1,0:T(8,128)S(1)}, f32[256,256]{1,0:T(8,128)S(1)}, u32[]{:S(2)}, u32[]{:S(2)}) collective-permute-start(f32[256,256]{1,0:T(8,128)S(1)} %get-tuple-element.37), channel_id=1, source_target_pairs={{0,1},{1,2},{2,3},{3,0},{4,5},{5,6},{6,7},{7,4},{8,9},{9,10},{10,1... | collective-permute-start | bytes 786440 | tf_op jit(solution)/shard_map/ppermute | solution.py:326
  138.5 0.0 collective-permute-start.18
  138.5 0.9 shard_map.45.partial
  139.4 3.9 %collective-permute-done.15.last_in = f32[256,256]{1,0:T(8,128)S(1)} collective-permute-done((f32[256,256]{1,0:T(8,128)S(1)}, f32[256,256]{1,0:T(8,128)S(1)}, u32[]{:S(2)}, u32[]{:S(2)}) %collective-permute-start.15) | collective-permute-done | bytes 262176 | tf_op jit(solution)/shard_map/ppermute | solution.py:322
  143.3 3.7 %collective-permute-done.17.col_in = f32[256,256]{1,0:T(8,128)S(1)} collective-permute-done((f32[256,256]{1,0:T(8,128)S(1)}, f32[256,256]{1,0:T(8,128)S(1)}, u32[]{:S(2)}, u32[]{:S(2)}) %collective-permute-start.17) | collective-permute-done | bytes 262176 | tf_op jit(solution)/shard_map/ppermute | solution.py:326
  147.0 5.9 %collective-permute-done.18.corner_in = f32[256,256]{1,0:T(8,128)S(1)} collective-permute-done((f32[256,256]{1,0:T(8,128)S(1)}, f32[256,256]{1,0:T(8,128)S(1)}, u32[]{:S(2)}, u32[]{:S(2)}) %collective-permute-start.18) | collective-permute-done | bytes 262176 | tf_op jit(solution)/shard_map/ppermute | solution.py:274
  152.9 0.0 collective-permute-done.16.others_in
  152.9 1.1 shard_map.46
  (6 shorter events, 0.2 us)
Async XLA Ops:
  0.0 12.7 %copy-start.1 = (f32[2,256,256]{2,1,0:T(8,128)S(1)}, f32[2,256,256]{2,1,0:T(8,128)}, u32[]{:S(2)}) copy-start(f32[2,256,256]{2,1,0:T(8,128)} %refs_2_.1) | copy-start | bytes 1572868
  1.2 19.5 %copy-start.2 = (s32[2,8,2]{1,2,0:T(2,128)S(1)}, s32[2,8,2]{1,2,0:T(2,128)}, u32[]{:S(2)}) copy-start(s32[2,8,2]{1,2,0:T(2,128)} %param.5) | copy-start | bytes 388
  1.2 8.8 %collective-permute-start.1 = (f32[256,256]{1,0:T(8,128)S(1)}, f32[256,256]{1,0:T(8,128)S(1)}, u32[]{:S(2)}, u32[]{:S(2)}) collective-permute-start(f32[256,256]{1,0:T(8,128)S(1)} %shard_map.37), channel_id=1, source_target_pairs={{0,8},{9,1},{18,26},{27,19},{4,20},{13,29},{22,6},{31,15}} | collective-permute-start | bytes 786440 | tf_op jit(solution)/shard_map/ppermute | solution.py:274
  10.0 40.4 %copy-start = (f32[512,1024]{1,0:T(8,128)S(1)}, f32[512,1024]{1,0:T(8,128)}, u32[]{:S(2)}) copy-start(f32[512,1024]{1,0:T(8,128)} %refs_1_.5) | copy-start | bytes 6291460
  10.0 5.4 %collective-permute-start.2 = (f32[256,256]{1,0:T(8,128)S(1)}, f32[256,256]{1,0:T(8,128)S(1)}, u32[]{:S(2)}, u32[]{:S(2)}) collective-permute-start(f32[256,256]{1,0:T(8,128)S(1)} %add.18), channel_id=1, source_target_pairs={{0,16},{8,24},{9,25},{1,17},{18,2},{26,10},{27,11},{19,3},{4,12},{... | collective-permute-start | bytes 786440 | tf_op jit(solution)/shard_map/ppermute | solution.py:274
  11.4 6.1 %collective-permute-start.4 = (f32[256,256]{1,0:T(8,128)S(1)}, f32[256,256]{1,0:T(8,128)S(1)}, u32[]{:S(2)}, u32[]{:S(2)}) collective-permute-start(f32[256,256]{1,0:T(8,128)S(1)} %shard_map.37), channel_id=1, source_target_pairs={{0,2},{4,6},{9,11},{13,15},{18,16},{22,20},{27,25},{31,29}} | collective-permute-start | bytes 786440 | tf_op jit(solution)/shard_map/ppermute | solution.py:274
  13.5 36.9 %collective-permute-start = (f32[256,256]{1,0:T(8,128)}, f32[256,256]{1,0:T(8,128)S(1)}, u32[]{:S(2)}, u32[]{:S(2)}) collective-permute-start(f32[256,256]{1,0:T(8,128)} %slice_bitcast_fusion), channel_id=1, source_target_pairs={{4,0},{9,5},{13,9},{18,14},{22,18},{27,23},{31,27},{0,28}} | collective-permute-start | bytes 786440 | tf_op jit(solution)/shard_map/ppermute | solution.py:274
  15.4 5.3 %collective-permute-start.3 = (f32[256,256]{1,0:T(8,128)S(1)}, f32[256,256]{1,0:T(8,128)}, u32[]{:S(2)}, u32[]{:S(2)}) collective-permute-start(f32[256,256]{1,0:T(8,128)S(1)} %add.19.refs_0_), channel_id=1, source_target_pairs={{0,4},{4,0},{8,12},{12,8},{16,20},{20,16},{24,28},{28,24},{1,5},{5... | collective-permute-start | bytes 786440 | tf_op jit(solution)/shard_map/ppermute | solution.py:314
  17.5 32.9 %collective-permute-start.5 = (f32[256,256]{1,0:T(8,128)S(1)}, f32[256,256]{1,0:T(8,128)}, u32[]{:S(2)}, u32[]{:S(2)}) collective-permute-start(f32[256,256]{1,0:T(8,128)S(1)} %add.20.refs_5_), channel_id=1, source_target_pairs={{0,1},{2,3},{4,5},{6,7},{9,8},{11,10},{13,12},{15,14},{18,19},{16,... | collective-permute-start | bytes 786440 | tf_op jit(solution)/shard_map/ppermute | solution.py:274
  67.7 5.2 %collective-permute-start.10 = (f32[256,256]{1,0:T(8,128)S(1)}, f32[256,256]{1,0:T(8,128)S(1)}, u32[]{:S(2)}, u32[]{:S(2)}) collective-permute-start(f32[256,256]{1,0:T(8,128)S(1)} %get-tuple-element.28), channel_id=1, source_target_pairs={{0,8},{9,1},{18,26},{27,19},{28,12},{5,21},{14,30},{23,7}} | collective-permute-start | bytes 786440 | tf_op jit(solution)/shard_map/ppermute | solution.py:274
  69.0 11.0 %collective-permute-start.8 = (f32[256,256]{1,0:T(8,128)S(1)}, f32[256,256]{1,0:T(8,128)S(1)}, u32[]{:S(2)}, u32[]{:S(2)}) collective-permute-start(f32[256,256]{1,0:T(8,128)S(1)} %get-tuple-element.27), channel_id=1, source_target_pairs={{3,1},{4,6},{8,10},{13,15},{17,19},{22,20},{26,24},{31,29}} | collective-permute-start | bytes 786440 | tf_op jit(solution)/shard_map/ppermute | solution.py:274
  72.9 10.8 %collective-permute-start.11 = (f32[256,256]{1,0:T(8,128)S(1)}, f32[256,256]{1,0:T(8,128)S(1)}, u32[]{:S(2)}, u32[]{:S(2)}) collective-permute-start(f32[256,256]{1,0:T(8,128)S(1)} %add.22), channel_id=1, source_target_pairs={{0,16},{8,24},{9,25},{1,17},{18,2},{26,10},{27,11},{19,3},{28,20},... | collective-permute-start | bytes 786440 | tf_op jit(solution)/shard_map/ppermute | solution.py:274
  77.0 51.1 %collective-permute-start.7 = (f32[256,512]{1,0:T(8,128)S(1)}, f32[256,512]{1,0:T(8,128)S(1)}, u32[]{:S(2)}, u32[]{:S(2)}) collective-permute-start(f32[256,512]{1,0:T(8,128)S(1)} %get-tuple-element.26), channel_id=1, source_target_pairs={{0,4},{4,8},{8,12},{12,16},{16,20},{20,24},{24,28},{28,0},{1,5},{5... | collective-permute-start | bytes 1572872 | tf_op jit(solution)/shard_map/ppermute | solution.py:322
  80.1 8.3 %collective-permute-start.9 = (f32[256,256]{1,0:T(8,128)S(1)}, f32[256,256]{1,0:T(8,128)S(1)}, u32[]{:S(2)}, u32[]{:S(2)}) collective-permute-start(f32[256,256]{1,0:T(8,128)S(1)} %add.21.refs_0_), channel_id=1, source_target_pairs={{3,2},{1,0},{4,5},{6,7},{8,9},{10,11},{13,12},{15,14},{17,16},{19,... | collective-permute-start | bytes 786440 | tf_op jit(solution)/shard_map/ppermute | solution.py:274
  83.8 4.9 %collective-permute-start.12 = (f32[256,256]{1,0:T(8,128)S(1)}, f32[256,256]{1,0:T(8,128)S(1)}, u32[]{:S(2)}, u32[]{:S(2)}) collective-permute-start(f32[256,256]{1,0:T(8,128)S(1)} %add.23.refs_2_), channel_id=1, source_target_pairs={{0,4},{4,0},{8,12},{12,8},{16,20},{20,16},{24,28},{28,24},{1,5},{5... | collective-permute-start | bytes 786440 | tf_op jit(solution)/shard_map/ppermute | solution.py:314
  84.1 44.0 %collective-permute-start.13 = (f32[256,256]{1,0:T(8,128)S(1)}, f32[256,256]{1,0:T(8,128)S(1)}, u32[]{:S(2)}, u32[]{:S(2)}) collective-permute-start(f32[256,256]{1,0:T(8,128)S(1)} %get-tuple-element.32), channel_id=1, source_target_pairs={{0,1},{1,2},{2,3},{3,0},{4,5},{5,6},{6,7},{7,4},{8,9},{9,10},{10,1... | collective-permute-start | bytes 786440 | tf_op jit(solution)/shard_map/ppermute | solution.py:326
  84.7 43.4 %collective-permute-start.14 = (f32[256,256]{1,0:T(8,128)S(1)}, f32[256,256]{1,0:T(8,128)S(1)}, u32[]{:S(2)}, u32[]{:S(2)}) collective-permute-start(f32[256,256]{1,0:T(8,128)S(1)} %get-tuple-element.33), channel_id=1, source_target_pairs={{0,5},{1,6},{2,7},{3,4},{4,9},{5,10},{6,11},{7,8},{8,13},{9,14},{1... | collective-permute-start | bytes 786440 | tf_op jit(solution)/shard_map/ppermute | solution.py:274
  88.4 44.7 %collective-permute-start.6 = (f32[256,256]{1,0:T(8,128)S(1)}, f32[256,256]{1,0:T(8,128)S(1)}, u32[]{:S(2)}, u32[]{:S(2)}) collective-permute-start(f32[256,256]{1,0:T(8,128)S(1)} %get-tuple-element.25), channel_id=1, source_target_pairs={{0,4},{4,8},{8,12},{12,16},{16,20},{20,24},{24,28},{28,0},{1,5},{5... | collective-permute-start | bytes 786440 | tf_op jit(solution)/shard_map/ppermute | solution.py:322
  130.9 22.0 %collective-permute-start.16 = (f32[256,512]{1,0:T(8,128)S(1)}, f32[256,512]{1,0:T(8,128)S(1)}, u32[]{:S(2)}, u32[]{:S(2)}) collective-permute-start(f32[256,512]{1,0:T(8,128)S(1)} %get-tuple-element.36), channel_id=1, source_target_pairs={{0,4},{4,8},{8,12},{12,16},{16,20},{20,24},{24,28},{28,0},{1,5},{5... | collective-permute-start | bytes 1572872 | tf_op jit(solution)/shard_map/ppermute | solution.py:322
  135.9 7.4 %collective-permute-start.15 = (f32[256,256]{1,0:T(8,128)S(1)}, f32[256,256]{1,0:T(8,128)S(1)}, u32[]{:S(2)}, u32[]{:S(2)}) collective-permute-start(f32[256,256]{1,0:T(8,128)S(1)} %get-tuple-element.35), channel_id=1, source_target_pairs={{0,4},{4,8},{8,12},{12,16},{16,20},{20,24},{24,28},{28,0},{1,5},{5... | collective-permute-start | bytes 786440 | tf_op jit(solution)/shard_map/ppermute | solution.py:322
  135.9 11.0 %collective-permute-start.17 = (f32[256,256]{1,0:T(8,128)S(1)}, f32[256,256]{1,0:T(8,128)S(1)}, u32[]{:S(2)}, u32[]{:S(2)}) collective-permute-start(f32[256,256]{1,0:T(8,128)S(1)} %get-tuple-element.37), channel_id=1, source_target_pairs={{0,1},{1,2},{2,3},{3,0},{4,5},{5,6},{6,7},{7,4},{8,9},{9,10},{10,1... | collective-permute-start | bytes 786440 | tf_op jit(solution)/shard_map/ppermute | solution.py:326
  138.5 14.4 %collective-permute-start.18 = (f32[256,256]{1,0:T(8,128)S(1)}, f32[256,256]{1,0:T(8,128)S(1)}, u32[]{:S(2)}, u32[]{:S(2)}) collective-permute-start(f32[256,256]{1,0:T(8,128)S(1)} %get-tuple-element.38), channel_id=1, source_target_pairs={{0,5},{1,6},{2,7},{3,4},{4,9},{5,10},{6,11},{7,8},{8,13},{9,14},{1... | collective-permute-start | bytes 786440 | tf_op jit(solution)/shard_map/ppermute | solution.py:274
